TPU v7x, 128 devices: a whole 4x4x4 slice. The times are simulated.
128 devices in a mesh: seq: 32 (over z, x, core), head: 4 (over y).
Axes of the slice: x: 4, y: 4, z: 4, core: 2. Of those that a mesh axis runs over, the one named last changes fastest.
Arguments:
- prompt_q: bfloat16 [32768, 2048], P('seq', 'head'), may hold values from -6 to 6
- prompt_k: bfloat16 [32768, 2048], P('seq', 'head'), may hold values from -6 to 6
- prompt_v: bfloat16 [32768, 2048], P('seq', 'head'), may hold values from -6 to 6
- prompt_grad: bfloat16 [32768, 2048], P('seq', 'head'), may hold values from -6 to 6
- cand_q: bfloat16 [16384, 2048], P('seq', 'head'), may hold values from -6 to 6
- cand_k: bfloat16 [16384, 2048], P('seq', 'head'), may hold values from -6 to 6
- cand_v: bfloat16 [16384, 2048], P('seq', 'head'), may hold values from -6 to 6
- readout: float32 [2048], P('head'), may hold values from -0.24 to 0.24
- prompt_ends: int32 [32], replicated, may hold values from 1 to 32768, as said below
- cand_lengths: int32 [32, 2], P('seq'), may hold values from 1 to 384, 512 in all within a row
- cand_prompt: int32 [64], replicated, may hold values from 0 to 31
- cand_ranks: int32 [64], replicated, may hold values from 0 to 3
Outputs:
- prompt_dq: bfloat16 [32768, 2048], P('seq', 'head')
- prompt_dk: bfloat16 [32768, 2048], P('seq', 'head')
- prompt_dv: bfloat16 [32768, 2048], P('seq', 'head')
- cand_dq: bfloat16 [16384, 2048], P('seq', 'head')
- cand_dk: bfloat16 [16384, 2048], P('seq', 'head')
- cand_dv: bfloat16 [16384, 2048], P('seq', 'head')
- list_loss: float32 [], replicated
Inputs may be any that keep to these rules, and one draw needn't show every extreme that they name: `prompt_ends`: strictly increasing; the last equals 32768; at most 2 ends lie in each range (d * 1024, (d + 1) * 1024], and in some range exactly 2. `cand_lengths`: each row sums to 512, and no entry exceeds 384.
All inputs are finite; a program needn't handle non-finite values.
Results may differ from a plain program's by a relative error of at most 0.0062.
Values may be sent and summed in bfloat16 or wider, within the bound.
A program may use at most 128 MiB of HBM per device.

v0:
```python
import math

import jax
import jax.numpy as jnp
from jax import lax
from jax.sharding import PartitionSpec as P

E = 128
ENDS = 2


grad_scale = 1048576.0


def prefix(part, axis, combine, identity, reverse):
    count = lax.axis_size(axis)
    place = lax.axis_index(axis)
    ahead = count - 1 - place if reverse else place
    gathered = jax.tree.map(lambda a: lax.all_gather(a, axis), part)
    state = jax.tree.map(lambda a, e: jnp.zeros_like(a) + jnp.asarray(e, a.dtype), part, identity)

    def one(lap, state):
        source = count - 1 - lap if reverse else lap
        return combine(
            state, jax.tree.map(lambda a: lax.dynamic_index_in_dim(a, source, 0, False), gathered)
        )

    return lax.fori_loop(0, ahead, one, state)


def pick_value(table, wanted):
    spots = jnp.arange(table.shape[0], dtype=jnp.int32)
    return jnp.sum(jnp.where(spots == wanted, table, 0))


def slab_layout(prompt_ends, slab_index, slab_width, slot_count):
    prompt_count = prompt_ends.shape[0]
    slab_start = slab_index * slab_width
    position = slab_start + jnp.arange(slab_width, dtype=jnp.int32)
    segment = jnp.sum((prompt_ends[None, :] <= position[:, None]).astype(jnp.int32), axis=1)
    begins = jnp.logical_or(slab_index == 0, jnp.any(prompt_ends == slab_start))
    first_seg = segment[0]
    last_seg = segment[slab_width - 1]
    first_end = jnp.sum((prompt_ends <= slab_start).astype(jnp.int32))
    slot_pid = first_end + jnp.arange(slot_count, dtype=jnp.int32)
    prompt_ids = jnp.arange(prompt_count, dtype=jnp.int32)
    slot_end = jnp.sum(
        jnp.where(prompt_ids[None, :] == slot_pid[:, None], prompt_ends[None, :], 0), axis=1
    )
    slot_valid = jnp.logical_and(slot_pid < prompt_count, slot_end <= slab_start + slab_width)
    slot_masks = jnp.logical_and(segment[None, :] == slot_pid[:, None], slot_valid[:, None])
    row_masks = jnp.concatenate([slot_masks, (segment == last_seg)[None, :]], axis=0)
    start_flag = jnp.logical_or(begins, first_seg != last_seg).astype(jnp.float32)
    end_flag = slot_valid[0].astype(jnp.float32)
    cont_right = (pick_value(prompt_ends, last_seg) != slab_start + slab_width).astype(jnp.float32)
    contin = 1.0 - begins.astype(jnp.float32)
    first_mask = segment == first_seg
    from_first = jnp.logical_and(slot_pid == first_seg, slot_valid).astype(jnp.float32)
    return (
        segment,
        row_masks,
        first_mask,
        contin,
        from_first,
        slot_pid,
        slot_valid,
        start_flag,
        end_flag,
        cont_right,
    )


def slot_rows(row_ids, prompt_ends, slab_width, slot_count):
    prompt_count = prompt_ends.shape[0]
    device_of = row_ids // slot_count
    slot_of = row_ids % slot_count
    first_end = jnp.sum(
        (prompt_ends[None, :] <= (device_of * slab_width)[:, None]).astype(jnp.int32), axis=1
    )
    row_pid = first_end + slot_of
    prompt_ids = jnp.arange(prompt_count, dtype=jnp.int32)
    row_end = jnp.sum(
        jnp.where(prompt_ids[None, :] == row_pid[:, None], prompt_ends[None, :], 0), axis=1
    )
    row_valid = jnp.logical_and(row_pid < prompt_count, row_end <= (device_of + 1) * slab_width)
    return (row_pid, row_valid)


def chain_combine(earlier, later):
    return (later[0] + (1.0 - later[1]) * earlier[0], jnp.maximum(earlier[1], later[1]))


def listwise(raw_scores, cand_prompt, cand_ranks, prompt_count):
    squashed = 3.0 * jnp.tanh(raw_scores)
    same_group = (cand_prompt[:, None] == cand_prompt[None, :]).astype(jnp.float32)
    exp_scores = jnp.exp(squashed)
    denoms = jnp.sum(same_group * exp_scores[None, :], axis=1)
    rank_weight = jnp.exp(-cand_ranks.astype(jnp.float32))
    targets = rank_weight / jnp.sum(same_group * rank_weight[None, :], axis=1)
    list_loss = -jnp.sum(targets * (squashed - jnp.log(denoms))) / prompt_count
    tanh_raw = jnp.tanh(raw_scores)
    raw_grad = (
        grad_scale
        / prompt_count
        * (exp_scores / denoms - targets)
        * 3.0
        * (1.0 - tanh_raw * tanh_raw)
    )
    return (list_loss, raw_grad)


def per_device(
    prompt_q,
    prompt_k,
    prompt_v,
    prompt_grad,
    cand_q,
    cand_k,
    cand_v,
    readout,
    prompt_ends,
    cand_lengths,
    cand_prompt,
    cand_ranks,
):
    slab_width = prompt_q.shape[0]
    cand_width = cand_q.shape[0]
    local_heads = prompt_q.shape[1] // E
    slab_count = lax.axis_size("seq")
    slab_index = lax.axis_index("seq")
    cand_count = cand_prompt.shape[0]
    per_slab = cand_lengths.shape[1]
    prompt_count = prompt_ends.shape[0]
    slot_count = ENDS
    scaling = 1.0 / math.sqrt(E * slab_width)
    queries = prompt_q.reshape(slab_width, local_heads, E)
    keys_in = prompt_k.reshape(slab_width, local_heads, E)
    values_in = prompt_v.reshape(slab_width, local_heads, E)
    grads_in = prompt_grad.reshape(slab_width, local_heads, E)
    cand_queries = cand_q.reshape(cand_width, local_heads, E)
    cand_keys = cand_k.reshape(cand_width, local_heads, E)
    cand_values = cand_v.reshape(cand_width, local_heads, E)
    readout_heads = readout.reshape(local_heads, E)
    (
        segment,
        row_masks,
        first_mask,
        contin,
        from_first,
        slot_pid,
        slot_valid,
        start_flag,
        end_flag,
        cont_right,
    ) = slab_layout(prompt_ends, slab_index, slab_width, slot_count)
    mask_rows = row_masks.astype(jnp.bfloat16)
    masked_keys = mask_rows[:, :, None, None] * keys_in[None]
    masked_values = mask_rows[:, :, None, None] * values_in[None]
    slab_sums = jnp.einsum(
        "mthd,the->mhde", masked_keys, values_in, preferred_element_type=jnp.float32
    )
    tail_state = slab_sums[slot_count]
    zero_state = jnp.zeros_like(tail_state)
    valid_float = slot_valid.astype(jnp.float32)
    lengths = cand_lengths[0]
    bounds = jnp.cumsum(lengths)
    tok_pos = jnp.arange(cand_width, dtype=jnp.int32)
    cand_id = jnp.sum((bounds[None, :] <= tok_pos[:, None]).astype(jnp.int32), axis=1)
    cand_masks = cand_id[None, :] == jnp.arange(per_slab, dtype=jnp.int32)[:, None]
    cand_float = cand_masks.astype(jnp.float32)
    cand_bf = cand_masks.astype(jnp.bfloat16)
    same_cand = jnp.logical_and(
        cand_id[:, None] == cand_id[None, :], tok_pos[None, :] <= tok_pos[:, None]
    )
    own_prompts = lax.dynamic_slice_in_dim(cand_prompt, slab_index * per_slab, per_slab)
    incoming, unused_flag = prefix(
        (tail_state, start_flag),
        "seq",
        chain_combine,
        (zero_state, jnp.zeros((), jnp.float32)),
        False,
    )
    incoming_first = contin * incoming
    end_slots = (
        slab_sums[:slot_count] + from_first[:, None, None, None] * incoming_first[None]
    ) * valid_float[:, None, None, None]
    shard_rows = lax.all_gather(end_slots.astype(jnp.bfloat16), "seq", axis=0, tiled=True)
    row_ids = jnp.arange(shard_rows.shape[0], dtype=jnp.int32)
    row_pid, row_valid = slot_rows(row_ids, prompt_ends, slab_width, slot_count)
    matches = jnp.logical_and(own_prompts[:, None] == row_pid[None, :], row_valid[None, :]).astype(
        jnp.bfloat16
    )
    cand_states = jnp.einsum(
        "jr,rhde->jhde", matches, shard_rows, preferred_element_type=jnp.float32
    ).astype(jnp.bfloat16)
    qk_scores = jnp.einsum(
        "thd,shd->hts", cand_queries, cand_keys, preferred_element_type=jnp.float32
    )
    attn_weights = jnp.where(same_cand[None], qk_scores, 0.0).astype(jnp.bfloat16)
    masked_queries = cand_bf[:, :, None, None] * cand_queries[None]
    outputs = scaling * (
        jnp.einsum("hts,she->the", attn_weights, cand_values, preferred_element_type=jnp.float32)
        + jnp.einsum(
            "jthd,jhde->the", masked_queries, cand_states, preferred_element_type=jnp.float32
        )
    )
    token_score = jnp.sum(jax.nn.silu(outputs) * readout_heads[None], axis=(1, 2))
    partial_raw = jnp.sum(cand_float * token_score[None, :], axis=1) / lengths.astype(jnp.float32)
    all_slots = jnp.arange(cand_count, dtype=jnp.int32)
    placed = jnp.where(all_slots // per_slab == slab_index, jnp.tile(partial_raw, slab_count), 0.0)
    raw_scores = lax.psum(placed, ("seq", "head"))
    list_loss, raw_grad = listwise(raw_scores, cand_prompt, cand_ranks, prompt_count)
    own_grad = lax.dynamic_slice_in_dim(raw_grad, slab_index * per_slab, per_slab) / lengths.astype(
        jnp.float32
    )
    token_coef = jnp.sum(cand_float * own_grad[:, None], axis=0)
    sigma = jax.nn.sigmoid(outputs)
    out_grad = (
        token_coef[:, None, None] * readout_heads[None] * sigma * (1.0 + outputs * (1.0 - sigma))
    ).astype(jnp.bfloat16)
    gv_scores = jnp.einsum(
        "the,she->hts", out_grad, cand_values, preferred_element_type=jnp.float32
    )
    grad_weights = jnp.where(same_cand[None], gv_scores, 0.0).astype(jnp.bfloat16)
    masked_grads = cand_bf[:, :, None, None] * out_grad[None]
    cand_dq = scaling * (
        jnp.einsum("hts,shd->thd", grad_weights, cand_keys, preferred_element_type=jnp.float32)
        + jnp.einsum(
            "jthe,jhde->thd", masked_grads, cand_states, preferred_element_type=jnp.float32
        )
    )
    cand_dk = scaling * jnp.einsum(
        "hts,thd->shd", grad_weights, cand_queries, preferred_element_type=jnp.float32
    )
    cand_dv = scaling * jnp.einsum(
        "hts,the->she", attn_weights, out_grad, preferred_element_type=jnp.float32
    )
    state_grads = (
        scaling
        * jnp.einsum("jthd,the->jhde", masked_queries, out_grad, preferred_element_type=jnp.float32)
    ).astype(jnp.bfloat16)
    row_ids = jnp.arange(lax.axis_size("seq") * slot_count, dtype=jnp.int32)
    row_pid, row_valid = slot_rows(row_ids, prompt_ends, slab_width, slot_count)
    matches = jnp.logical_and(row_pid[:, None] == own_prompts[None, :], row_valid[:, None]).astype(
        jnp.bfloat16
    )
    slot_grads = lax.psum_scatter(
        jnp.einsum("rj,jhde->rhde", matches, state_grads, preferred_element_type=jnp.float32),
        "seq",
        scatter_dimension=0,
        tiled=True,
    )
    slot_grads = slot_grads * valid_float[:, None, None, None]
    first_bf = first_mask.astype(jnp.bfloat16)
    head_state = (
        scaling
        * jnp.einsum(
            "thd,the->hde",
            first_bf[:, None, None] * queries,
            grads_in,
            preferred_element_type=jnp.float32,
        )
        + end_flag * slot_grads[0]
    )
    from_right, unused_back = prefix(
        (head_state, end_flag), "seq", chain_combine, (zero_state, jnp.zeros((), jnp.float32)), True
    )
    right_states = jnp.concatenate([slot_grads, (cont_right * from_right)[None]], axis=0).astype(
        jnp.bfloat16
    )
    incoming_bf = incoming_first.astype(jnp.bfloat16)
    slab_pos = jnp.arange(slab_width, dtype=jnp.int32)
    same_prompt = jnp.logical_and(
        segment[:, None] == segment[None, :], slab_pos[None, :] <= slab_pos[:, None]
    )
    attn_prompt = jnp.where(
        same_prompt[None],
        jnp.einsum("thd,shd->hts", queries, keys_in, preferred_element_type=jnp.float32),
        0.0,
    ).astype(jnp.bfloat16)
    grad_prompt = jnp.where(
        same_prompt[None],
        jnp.einsum("the,she->hts", grads_in, values_in, preferred_element_type=jnp.float32),
        0.0,
    ).astype(jnp.bfloat16)
    first_float = first_mask.astype(jnp.float32)
    prompt_dq = scaling * (
        jnp.einsum("hts,shd->thd", grad_prompt, keys_in, preferred_element_type=jnp.float32)
        + first_float[:, None, None]
        * jnp.einsum("the,hde->thd", grads_in, incoming_bf, preferred_element_type=jnp.float32)
    )
    prompt_dk = scaling * jnp.einsum(
        "hts,thd->shd", grad_prompt, queries, preferred_element_type=jnp.float32
    ) + jnp.einsum(
        "mshe,mhde->shd", masked_values, right_states, preferred_element_type=jnp.float32
    )
    prompt_dv = scaling * jnp.einsum(
        "hts,the->she", attn_prompt, grads_in, preferred_element_type=jnp.float32
    ) + jnp.einsum("mshd,mhde->she", masked_keys, right_states, preferred_element_type=jnp.float32)
    flat_width = local_heads * E
    return (
        prompt_dq.astype(jnp.bfloat16).reshape(slab_width, flat_width),
        prompt_dk.astype(jnp.bfloat16).reshape(slab_width, flat_width),
        prompt_dv.astype(jnp.bfloat16).reshape(slab_width, flat_width),
        cand_dq.astype(jnp.bfloat16).reshape(cand_width, flat_width),
        cand_dk.astype(jnp.bfloat16).reshape(cand_width, flat_width),
        cand_dv.astype(jnp.bfloat16).reshape(cand_width, flat_width),
        list_loss,
    )


def solution(mesh):
    return jax.shard_map(
        per_device,
        mesh=mesh,
        in_specs=(
            P("seq", "head"),
            P("seq", "head"),
            P("seq", "head"),
            P("seq", "head"),
            P("seq", "head"),
            P("seq", "head"),
            P("seq", "head"),
            P("head"),
            P(),
            P("seq", None),
            P(),
            P(),
        ),
        out_specs=(
            P("seq", "head"),
            P("seq", "head"),
            P("seq", "head"),
            P("seq", "head"),
            P("seq", "head"),
            P("seq", "head"),
            P(),
        ),
        check_vma=False,
    )
```

profile of v0, /device:TPU:1, one launch (start us, length us, event | category | flops | bytes accessed | tf_op | source)
XLA Modules:
  0.0 632.4 jit_solution(2478453898907527330)
XLA Ops:
  8.7 1.9 fusion.93
  12.1 1.3 fusion.107
  13.4 1.3 and_convert_fusion
  15.0 1.7 reshape.355
  16.8 1.6 fusion.38
  24.8 65.7 %all-reduce.3 = (f32[32]{0:T(128)S(1)}, f32[32]{0:T(128)S(1)}) all-reduce(f32[32]{0:T(128)S(1)} %dynamic-update-slice, f32[32]{0:T(128)S(1)} %fusion.102), channel_id=1, replica_groups=mesh['seq'=32,'head'=4] {'seq'}, use_global_device_ids=true, to_apply=%add | all-reduce | flops 64 | bytes 512
  90.5 2.3 while.26
  91.8 1.1 bitcast_add_fusion.7
  94.0 1.3 copy.175
  96.0 2.1 select_convert_fusion.3
  98.1 118.4 %all-gather.7.cloned.1.call-done = bf16[64,4,128,128]{3,2,0,1:T(8,128)(2,1)} async-done(((bf16[2,4,128,128]{3,2,0,1:T(8,128)(2,1)}), bf16[64,4,128,128]{3,2,0,1:T(8,128)(2,1)}) %all-gather.7.cloned.1.call-update) | async-done | bytes 8388624 | tf_op jit(solution)/shard_map/all_gather | solution.py:187
  216.4 8.1 %fusion.44 = bf16[2,4,128,128]{3,0,2,1:T(2,128)(2,1)S(1)} fusion(bf16[64,4,128,128]{3,2,0,1:T(8,128)(2,1)} %all-gather.7.cloned.1.call-done, pred[64]{0:T(512)(128)(4,1)S(1)} %compare_and_fusion.1, s32[64]{0:T(128)S(1)} %fusion.91, s32[2]{0:T(128)S(1)} %dynamic_slice.32), kind=kOutput, calls=%fused_computation.49 | convolution fusion | flops 16908544 | bytes 8651080 | tf_op jit(solution)/shard_map/jr,rhde->jhde/dot_general | solution.py:193
  225.3 1.9 multiply_reduce_fusion
  227.4 64.6 %psum.7 = f32[64]{0:T(128)S(1)} all-reduce(f32[64]{0:T(128)S(1)} %compare_select_fusion.3), channel_id=1, replica_groups=mesh['seq'=32,'head'=4] {'seq','head'}, use_global_device_ids=true, to_apply=%region_12.13 | all-reduce | flops 64 | bytes 512 | tf_op jit(solution)/shard_map/psum | solution.py:211
  293.1 1.7 multiply_convert_fusion
  295.5 2.5 fusion.82
  297.9 11.7 %copy.137 = f32[64,4,128,128]{3,2,0,1:T(8,128)} copy(f32[64,4,128,128]{3,0,2,1:T(8,128)S(1)} %fusion.82) | data formatting | bytes 33554432 | tf_op jit(solution)/shard_map/rj,jhde->rhde/dot_general | solution.py:248
  310.2 1.5 copy.173
  311.7 2.3 copy.174
  314.7 169.4 %all-reduce.6.cloned.1.call-done = f32[64,4,128,128]{3,2,0,1:T(8,128)} async-done(((f32[64,4,128,128]{3,2,0,1:T(8,128)}), f32[64,4,128,128]{3,2,0,1:T(8,128)}) %all-reduce.6.cloned.1.call-update) | async-done | bytes 16777232
  484.0 1.9 fusion.106
  485.9 2.9 fusion.53
  489.5 2.5 copy_bitcast_fusion.1
  492.6 2.7 select_convert_fusion.1
  495.3 3.2 copy-done.1
  498.6 2.6 fusion.110
  501.2 6.9 %fusion.9 = f32[4,1024,128]{1,2,0:T(8,128)} fusion(bf16[1024,4,128]{0,2,1:T(8,128)(2,1)S(1)} %bitcast.199, bf16[1024,4,128]{0,2,1:T(8,128)(2,1)} %bitcast.203, pred[1024,1024]{1,0:T(8,128)(4,1)} %copy-done.11, bf16[1024,512]{1,0:T(8,128)(2,1)S(1)} %copy-done), kind=kOutput, calls=%fused_computation.16 | convolution fusion | flops 2155872256 | bytes 6291456 | tf_op jit(solution)/shard_map/hts,the->she/dot_general | solution.py:297
  508.1 6.3 %fusion.104 = f32[4,1024,128]{1,2,0:T(8,128)S(1)} fusion(bf16[4,1024,1024]{2,1,0:T(8,128)(2,1)} %copy-done.1, bf16[1024,512]{1,0:T(8,128)(2,1)S(1)} %copy-done), kind=kOutput, calls=%fused_computation.154 | convolution fusion | flops 1073741824 | bytes 11534336 | tf_op jit(solution)/shard_map/hts,shd->thd/dot_general | solution.py:288
  514.4 1.4 fusion.13
  515.9 2.3 copy.151
  519.1 2.0 select_convert_fusion.2
  521.2 1.6 fusion.35
  522.8 2.0 copy.154
  524.8 3.1 fusion.36
  528.0 2.0 copy.156
  530.0 2.4 fusion.37
  532.4 2.2 copy.155
  535.2 7.7 %all-gather.9.cloned.1.call-done = f32[128,128,128]{2,1,0:T(8,128)} async-done(((f32[4,128,128]{2,1,0:T(8,128)}), f32[128,128,128]{2,1,0:T(8,128)}) %all-gather.9.cloned.1.call-update) | async-done | bytes 8388624 | tf_op jit(solution)/shard_map/all_gather | solution.py:19
  542.9 69.5 %while.27 = (s32[]{:T(128)}, f32[4,128,128]{2,1,0:T(8,128)S(1)}, s32[]{:T(128)}, f32[32,4,128,128]{3,2,1,0:T(8,128)}, f32[32]{0:T(128)S(1)}, /*index=5*/s32[]{:T(128)}, s32[]{:T(128)}, s32[]{:T(128)}, s32[]{:T(128)}, f32[1]{0:T(128)}) while((s32[]{:T(128)}, f32[4,128,128]{2,1,0:T(8,128)S(1)}, s32[]{:T(128)}, ...), condition=%wide.region_19.20_spmd, body=%wide.region_18.19_spmd.sunk | while | flops 131079 | bytes 786611 | solution.py:28
  544.2 1.0 bitcast_add_fusion.8
  546.5 1.0 bitcast_add_fusion.8
  548.8 1.0 bitcast_add_fusion.8
  551.2 1.0 bitcast_add_fusion.8
  553.5 1.0 bitcast_add_fusion.8
  555.8 1.0 bitcast_add_fusion.8
  558.1 1.0 bitcast_add_fusion.8
  560.4 1.0 bitcast_add_fusion.8
  565.1 1.0 bitcast_add_fusion.8
  569.7 1.0 bitcast_add_fusion.8
  574.3 1.0 bitcast_add_fusion.8
  578.9 1.0 bitcast_add_fusion.8
  583.6 1.0 bitcast_add_fusion.8
  588.2 1.0 bitcast_add_fusion.8
  590.5 1.0 bitcast_add_fusion.8
  592.8 1.0 bitcast_add_fusion.8
  595.2 1.0 bitcast_add_fusion.8
  597.5 1.0 bitcast_add_fusion.8
  599.8 1.0 bitcast_add_fusion.8
  602.1 1.0 bitcast_add_fusion.8
  604.4 1.0 bitcast_add_fusion.8
  612.5 4.2 fusion.10
  616.7 2.3 copy.153
  618.9 3.6 fusion.11
  622.5 2.3 copy.152
  (149 shorter events, 41.7 us)
Async XLA Ops:
  7.2 7.6 %copy-start = (bf16[1024,512]{1,0:T(8,128)(2,1)S(1)}, bf16[1024,512]{1,0:T(8,128)(2,1)}, u32[]{:S(2)}) copy-start(bf16[1024,512]{1,0:T(8,128)(2,1)} %param.17) | copy-start | bytes 3145732
  7.2 83.2 %all-gather.5.cloned.1.call-start = ((), (), s32[]{:S(2)}) async-start(), calls=%async_computation | async-start | bytes 8650752 | tf_op jit(solution)/shard_map/all_gather | solution.py:19
  15.0 3.4 copy-start.10
  16.8 4.7 copy-start.18
  16.8 6.0 copy-start.20
  18.4 0.9 copy-start.12
  20.0 72.8 %copy-start.13 = (f32[3,4,128,128]{3,2,0,1:T(8,128)S(1)}, f32[3,4,128,128]{3,2,0,1:T(8,128)}, u32[]{:S(2)}) copy-start(f32[3,4,128,128]{3,2,0,1:T(8,128)} %copy-done.12) | copy-start | bytes 2359300
  20.0 196.4 %all-gather.7.cloned.1.call-start = ((), (), s32[]{:S(2)}) async-start(), calls=%async_computation.1 | async-start | bytes 8650752 | tf_op jit(solution)/shard_map/all_gather | solution.py:187
  23.4 70.4 %copy-start.22 = (s32[1,2]{1,0:T(1,128)S(1)}, s32[1,2]{1,0:T(1,128)}, u32[]{:S(2)}) copy-start(s32[1,2]{1,0:T(1,128)} %param.25) | copy-start | bytes 28
  90.5 4.8 copy-start.19
  90.5 5.2 copy-start.21
  90.5 5.4 copy-start.6
  93.7 390.3 %all-reduce.6.cloned.1.call-start = ((), (), s32[]{:S(2)}) async-start(), calls=%async_computation.3 | async-start | bytes 33554432
  95.2 2.8 copy-start.8
  95.9 128.7 %copy-start.14 = (pred[512,512]{1,0:T(8,128)(4,1)}, pred[512,512]{1,0:T(8,128)(4,1)S(1)}, u32[]{:S(2)}) copy-start(pred[512,512]{1,0:T(8,128)(4,1)S(1)} %fusion.57) | copy-start | bytes 786436
  98.0 127.2 %copy-start.17 = (f32[512]{0:T(512)S(1)}, f32[512]{0:T(512)}, u32[]{:S(2)}) copy-start(f32[512]{0:T(512)} %param.23) | copy-start | bytes 6148
  98.0 127.2 %copy-start.23 = (bf16[512,512]{1,0:T(8,128)(2,1)S(1)}, bf16[512,512]{1,0:T(8,128)(2,1)}, u32[]{:S(2)}) copy-start(bf16[512,512]{1,0:T(8,128)(2,1)} %param.22) | copy-start | bytes 1572868
  216.4 8.8 %copy-start.5 = (bf16[4,512,512]{2,1,0:T(8,128)(2,1)S(1)}, bf16[4,512,512]{2,1,0:T(8,128)(2,1)}, u32[]{:S(2)}) copy-start(bf16[4,512,512]{2,1,0:T(8,128)(2,1)} %select_convert_fusion.3) | copy-start | bytes 6291460
  294.8 223.4 %copy-start.2 = (bf16[512,4,128]{0,2,1:T(8,128)(2,1)}, bf16[512,4,128]{0,2,1:T(8,128)(2,1)S(1)}, u32[]{:S(2)}) copy-start(bf16[512,4,128]{0,2,1:T(8,128)(2,1)S(1)} %multiply_convert_fusion) | copy-start | bytes 1572868
  309.7 233.3 %all-gather.9.cloned.1.call-start = ((), (), s32[]{:S(2)}) async-start(), calls=%async_computation.2 | async-start | bytes 8650752 | tf_op jit(solution)/shard_map/all_gather | solution.py:19
  489.5 3.1 copy-start.3
  492.6 2.7 copy-start.11
  492.6 5.9 copy-start.4
  495.3 3.2 copy-start.1
  515.9 3.2 copy-start.15
  518.5 2.7 copy-start.9
  532.4 80.1 %copy-start.16 = (bf16[2,4,128,128]{3,2,0,1:T(8,128)(2,1)S(1)}, bf16[2,4,128,128]{3,2,0,1:T(8,128)(2,1)}, u32[]{:S(2)}) copy-start(bf16[2,4,128,128]{3,2,0,1:T(8,128)(2,1)} %get-tuple-element.213) | copy-start | bytes 786436
  612.5 6.5 %copy-start.7 = (f32[4,1024,128]{1,2,0:T(8,128)S(1)}, f32[4,1024,128]{1,2,0:T(8,128)}, u32[]{:S(2)}) copy-start(f32[4,1024,128]{1,2,0:T(8,128)} %fusion.110) | copy-start | bytes 6291460
Sparse Core Ops, SparseCore 0:
  20.2 56.6 all-gather.4
  93.9 122.5 all-gather.6
  309.8 174.1 all-reduce.5
  489.0 53.8 all-gather.8
where the time goes:
time: 636 us; the launch traced here: 632 us
  waiting for transfers between devices  296 us (47%)
  blocking collectives  130 us (20%)
  local copies, waits for them, and re-layouts  60 us (9%)
  matrix products  57.8 us (9%)
  other arithmetic  48.1 us (8%)
  loops' own time  21.1 us (3%)
  between operations  19.4 us (3%)
    unnamed x5, waiting for transfers between devices  169 us
    all_gather x1, waiting for transfers between devices, per_device(): lax.all_gather(end_slots.astype(jnp.bfloat16), 'seq', axis=0, tiled=True)  118 us
    unnamed x1, blocking collectives  65.7 us
    psum x1, blocking collectives, per_device(): raw_scores = lax.psum(placed, ('seq', 'head'))  64.6 us
    add x31, other arithmetic, chain_combine(): later[0] + (1.0 - later[1]) * earlier[0]  32.5 us
    another operation x2, loops' own time, prefix(): return lax.fori_loop(0, ahead, one, state)  21.1 us
    unnamed x58, local copies, waits for them, and re-layouts  18.6 us
    dynamic_slice x31, local copies, waits for them, and re-layouts, one(): lax.dynamic_index_in_dim(a, source, 0, False)  18.2 us
  transfers between devices with their start and end apart: 4, of which 3 were waited for; matrix products, arithmetic and copies ran while one was open for 8% of the time, Pallas kernels for 0%

commit v1 on v0

v1 whole, which is shorter than its diff:
```python
import functools
import math

import jax
import jax.numpy as jnp
from jax import lax
from jax.experimental import pallas as pl
from jax.experimental.pallas import tpu as pltpu
from jax.sharding import PartitionSpec as P

E = 128
LOCAL_HEADS = 4
HALF = LOCAL_HEADS // 2
RING = 4
CHUNK = 256
PIECES = 3
FAR = 1 << 30
GRAD_SCALE = 1048576.0
MESH = pl.DeviceIdType.MESH
BF = jnp.bfloat16
F32 = jnp.float32

VMEM_SPEC = pl.BlockSpec(memory_space=pltpu.VMEM)
SMEM_SPEC = pl.BlockSpec(memory_space=pltpu.SMEM)


def dot_nn(a, b):
    return lax.dot_general(a, b, (((1,), (0,)), ((), ())), preferred_element_type=F32)


def dot_nt(a, b):
    return lax.dot_general(a, b, (((1,), (1,)), ((), ())), preferred_element_type=F32)


def dot_tn(a, b):
    return lax.dot_general(a, b, (((0,), (0,)), ((), ())), preferred_element_type=F32)


def local_ends(meta_ref, ends_ref, slab, width, count):
    first = meta_ref[slab]
    last = ends_ref.shape[0] - 1
    end0 = ends_ref[jnp.minimum(first, last)] - slab * width
    end1 = jnp.where(
        first + 1 <= last, ends_ref[jnp.minimum(first + 1, last)] - slab * width, FAR
    )
    return end0, end1


class Place:
    def __init__(self):
        self.seq = lax.axis_index("seq")
        self.head = lax.axis_index("head")
        self.core = self.seq % 2
        x = (self.seq // 2) % RING
        z = self.seq // (2 * RING)
        self.pos_a = z * (1 - self.core) + x * self.core
        self.pos_b = x * (1 - self.core) + z * self.core
        self.step_a = 8 - 6 * self.core
        self.step_b = 2 + 6 * self.core

    def chip_at(self, move_a, move_b):
        return ((self.pos_a + move_a) % RING) * self.step_a + (
            (self.pos_b + move_b) % RING
        ) * self.step_b

    def neighbour(self, move_a, move_b):
        return (self.chip_at(move_a, move_b) + self.core, self.head)

    def partner(self):
        return (self.seq + 1 - 2 * self.core, self.head)

    def friends(self):
        return (
            self.neighbour(1, 0),
            self.neighbour(RING - 1, 0),
            self.neighbour(0, 1),
            self.neighbour(0, RING - 1),
            self.partner(),
        )


ROUTE_COPIES = 14


def route_scratch(slots, rows_out):
    return [
        pltpu.VMEM((RING, 2, slots, HALF, E, E), BF),
        pltpu.VMEM((RING, 2, rows_out, HALF, E, E), BF),
        pltpu.VMEM((4, rows_out, HALF, E, E), F32),
        pltpu.VMEM((2, rows_out, HALF, E, E), BF),
        pltpu.VMEM((2, 2, rows_out, HALF, E, E), BF),
        pltpu.VMEM((2, rows_out, HALF, E, E), BF),
        pltpu.VMEM((rows_out, HALF, E, E), BF),
        pltpu.SemaphoreType.DMA((ROUTE_COPIES,)),
        pltpu.SemaphoreType.DMA((ROUTE_COPIES,)),
        pltpu.SemaphoreType.DMA((1,)),
    ]


def route(place, rows_ref, rows_in, rows_out, slots, pick, scratch, between, sum_slot, zero_slot):
    gathered, parts, exact, passed, arrived, final, swapped, send, recv, local = scratch
    core = place.core
    left_a, right_a = place.neighbour(RING - 1, 0), place.neighbour(1, 0)
    left_b, right_b = place.neighbour(0, RING - 1), place.neighbour(0, 1)
    partner = place.partner()

    def remote(at, src, dst, device):
        return pltpu.make_async_remote_copy(
            src_ref=src,
            dst_ref=dst,
            send_sem=send.at[at],
            recv_sem=recv.at[at],
            device_id=device,
            device_id_type=MESH,
        )

    slot_rows = pl.ds(0, rows_in)
    mine = pltpu.make_async_copy(
        rows_ref.at[:, pl.ds(HALF * core, HALF)], gathered.at[0, core, slot_rows], local.at[0]
    )
    swap = remote(
        0,
        rows_ref.at[:, pl.ds(HALF * (1 - core), HALF)],
        gathered.at[0, core, slot_rows],
        partner,
    )
    mine.start()
    swap.start()
    for k in range(RING):
        for cc in range(2):
            gathered[k, cc, zero_slot] = jnp.zeros((HALF, E, E), BF)
    mine.wait()
    swap.wait()

    def block(k, cc):
        return gathered.at[k, cc, slot_rows]

    to_left = [remote(1 + cc, block(0, cc), block(1, cc), left_a) for cc in range(2)]
    to_right = [remote(3 + cc, block(0, cc), block(3, cc), right_a) for cc in range(2)]
    to_left[0].start()
    to_right[1].start()
    to_left[1].start()
    to_right[0].start()
    on_left = remote(5, block(1, 0), block(2, 0), left_a)
    on_right = remote(6, block(3, 1), block(2, 1), right_a)
    between(0)
    to_left[0].wait_recv()
    on_left.start()
    to_right[1].wait_recv()
    on_right.start()
    between(1)
    to_left[1].wait_recv()
    to_right[0].wait_recv()
    on_left.wait_recv()
    on_right.wait_recv()
    for copy in to_left + to_right + [on_left, on_right]:
        copy.wait_send()

    if sum_slot is not None:
        for k in range(RING):
            for cc in range(2):
                gathered[k, cc, sum_slot] = (
                    gathered[k, cc, 0].astype(F32) + gathered[k, cc, 1].astype(F32)
                ).astype(BF)

    def combine(m, cd, keep=None):
        dest = place.chip_at(0, m) + cd
        for r in range(rows_out):
            total = None
            for k in range(RING):
                for cc in range(2):
                    src = place.chip_at(k, 0) + cc
                    term = gathered[k, cc, pick(src, dest, r)].astype(F32)
                    total = term if total is None else total + term
            if keep is None:
                parts[m, cd, r] = total.astype(BF)
            else:
                exact[keep, r] = total

    far_left = remote(7, parts.at[2, 0], passed.at[0], left_b)
    far_right = remote(8, parts.at[2, 1], passed.at[1], right_b)
    left_own = remote(9, parts.at[3, 1], arrived.at[0, 1], left_b)
    right_own = remote(10, parts.at[1, 0], arrived.at[1, 0], right_b)
    left_sum = remote(11, parts.at[3, 0], arrived.at[0, 0], left_b)
    right_sum = remote(12, parts.at[1, 1], arrived.at[1, 1], right_b)
    combine(2, 0)
    far_left.start()
    combine(2, 1)
    far_right.start()
    combine(3, 1)
    left_own.start()
    combine(1, 0)
    right_own.start()
    combine(3, 0, keep=2)
    combine(1, 1, keep=3)
    far_left.wait_recv()
    parts[3, 0] = (exact[2] + passed[0].astype(F32)).astype(BF)
    left_sum.start()
    far_right.wait_recv()
    parts[1, 1] = (exact[3] + passed[1].astype(F32)).astype(BF)
    right_sum.start()
    combine(0, 0, keep=0)
    combine(0, 1, keep=1)
    between(2)
    for copy in (left_own, right_own, left_sum, right_sum):
        copy.wait_recv()
    final[...] = (
        exact[:2] + arrived[0].astype(F32) + arrived[1].astype(F32)
    ).astype(BF)
    back = remote(13, final.at[1 - core], swapped, partner)
    back.start()
    for copy in (far_left, far_right, left_own, right_own, left_sum, right_sum):
        copy.wait_send()
    back.wait()


def greet(devices):
    barrier = pltpu.get_barrier_semaphore()
    for device in devices:
        pl.semaphore_signal(barrier, inc=1, device_id=device, device_id_type=MESH)


def pieces_kernel(meta_ref, ends_ref, q_ref, k_ref, v_ref, g_ref, out_ref):
    width = q_ref.shape[0]
    slab = lax.axis_index("seq")
    end0, end1 = local_ends(meta_ref, ends_ref, slab, width, PIECES)
    spot = lax.broadcasted_iota(jnp.int32, (width, 1), 0)
    v = v_ref[...]
    zero = jnp.zeros_like(v)
    split = jnp.concatenate(
        [
            jnp.where(spot < end0, v, zero),
            jnp.where(jnp.logical_and(spot >= end0, spot < end1), v, zero),
            jnp.where(spot >= end1, v, zero),
        ],
        axis=1,
    )
    sums = dot_tn(k_ref[...], split)
    for j in range(PIECES):
        out_ref[j, 0] = sums[:, j * E : (j + 1) * E].astype(BF)
    scaling = 1.0 / math.sqrt(E * width)
    out_ref[PIECES, 0] = (
        scaling * dot_tn(q_ref[...], jnp.where(spot < end0, g_ref[...], zero))
    ).astype(BF)


def forward_kernel(meta_ref, cand_ref, rows_ref, out_ref, *scratch):
    place = Place()
    slabs = meta_ref.shape[0] // 2
    friends = place.friends()
    greet(friends)
    pl.semaphore_wait(pltpu.get_barrier_semaphore(), len(friends))

    def pick(src, dest, r):
        first = meta_ref[src]
        if r < 2:
            wanted = cand_ref[2 * dest + r]
            ok = jnp.bool_(True)
        elif r == 2:
            wanted = meta_ref[dest]
            ok = src < dest
        else:
            wanted = meta_ref[slabs + dest]
            same = jnp.logical_and(first == wanted, src > dest)
            return jnp.where(same, 3, 4)
        j = wanted - first
        found = jnp.logical_and(jnp.logical_and(j >= 0, j < PIECES), ok)
        return jnp.where(found, j, 4)

    route(place, rows_ref, 4, 4, 5, pick, scratch, lambda at: None, None, 4)
    final, swapped = scratch[5], scratch[6]
    out_ref[:, pl.ds(HALF * place.core, HALF)] = final[place.core]
    out_ref[:, pl.ds(HALF * (1 - place.core), HALF)] = swapped[...]


def cand_kernel(
    meta_ref,
    cand_ref,
    lens_ref,
    states_ref,
    q_ref,
    k_ref,
    v_ref,
    readout_ref,
    table_ref,
    dq_ref,
    dk_ref,
    dv_ref,
    right_ref,
    loss_ref,
    attn_ref,
    outs_ref,
    dout_ref,
    grads_ref,
    mine_ref,
    heads_ref,
    total_ref,
    scores_ref,
    y_send,
    y_recv,
    s_send,
    s_recv,
    *scratch,
):
    place = Place()
    slabs = meta_ref.shape[0] // 2
    planes = lax.axis_size("head")
    width = q_ref.shape[0]
    scaling = 1.0 / math.sqrt(E * 2 * width)
    barrier = pltpu.get_barrier_semaphore()

    def other_slab(at):
        return (place.seq + at) % slabs, place.head

    def hello(at, carry):
        pl.semaphore_signal(barrier, inc=1, device_id=other_slab(at), device_id_type=MESH)
        return carry

    lax.fori_loop(1, slabs, hello, 0)
    planes_other = [(place.seq, (place.head + at) % planes) for at in range(1, planes)]
    greet(planes_other)

    len0 = lens_ref[0, 0]
    len1 = lens_ref[0, 1]
    row = lax.broadcasted_iota(jnp.int32, (width, 1), 0)
    in_second = row >= len0

    def mask_of(rows, columns):
        i = lax.broadcasted_iota(jnp.int32, (width, width), 0)
        j = lax.broadcasted_iota(jnp.int32, (width, width), 1)
        apart = jnp.logical_and(i >= len0, j < len0)
        return jnp.logical_and(j <= i, jnp.logical_not(apart))

    sum_all = jnp.zeros((1, E), F32)
    sum_second = jnp.zeros((1, E), F32)
    for h in range(LOCAL_HEADS):
        cols = slice(h * E, (h + 1) * E)
        q, k, v = q_ref[:, cols], k_ref[:, cols], v_ref[:, cols]
        attn = jnp.where(mask_of(width, width), dot_nt(q, k), 0.0).astype(BF)
        attn_ref[h] = attn
        far = jnp.where(in_second, dot_nn(q, states_ref[1, h]), dot_nn(q, states_ref[0, h]))
        out = scaling * (dot_nn(attn, v) + far)
        outs_ref[h] = out
        part = out / (1.0 + jnp.exp(-out)) * readout_ref[:, cols]
        sum_all = sum_all + jnp.sum(part, axis=0, keepdims=True)
        sum_second = sum_second + jnp.sum(
            jnp.where(in_second, part, 0.0), axis=0, keepdims=True
        )
    second = jnp.sum(sum_second, axis=1, keepdims=True)
    first = jnp.sum(sum_all - sum_second, axis=1, keepdims=True)
    lane = lax.broadcasted_iota(jnp.int32, (1, E), 1)
    mine_ref[...] = jnp.where(
        lane == 0,
        first / len0.astype(F32),
        jnp.where(lane == 1, second / len1.astype(F32), 0.0),
    )
    pl.semaphore_wait(barrier, slabs - 1 + planes - 1)

    to_planes = [
        pltpu.make_async_remote_copy(
            src_ref=mine_ref,
            dst_ref=heads_ref.at[place.head],
            send_sem=y_send.at[at],
            recv_sem=y_recv.at[at],
            device_id=device,
            device_id_type=MESH,
        )
        for at, device in enumerate(planes_other)
    ]
    for copy in to_planes:
        copy.start()
    heads_ref[place.head] = mine_ref[...]
    for copy in to_planes:
        copy.wait()
    total = heads_ref[0]
    for at in range(1, planes):
        total = total + heads_ref[at]
    total_ref[...] = total

    def score_copy(at):
        return pltpu.make_async_remote_copy(
            src_ref=total_ref,
            dst_ref=scores_ref.at[place.seq],
            send_sem=s_send.at[at],
            recv_sem=s_recv.at[at],
            device_id=other_slab(at),
            device_id_type=MESH,
        )

    def tell(at, carry):
        score_copy(at).start()
        return carry

    def told(at, carry):
        score_copy(at).wait()
        return carry

    lax.fori_loop(1, slabs, tell, 0)
    scores_ref[place.seq] = total
    lax.fori_loop(1, slabs, told, 0)

    raw = scores_ref[...].reshape(slabs, E)
    prompts = lax.broadcasted_iota(jnp.int32, (slabs, E), 1)
    tanh_raw = jnp.tanh(raw)
    squashed = 3.0 * tanh_raw
    exp_scores = jnp.exp(squashed)
    table = table_ref[...]
    hot = [(table[:, j : j + 1] == prompts).astype(F32) for j in range(2)]
    weight = [jnp.exp(-table[:, 2 + j : 3 + j].astype(F32)) for j in range(2)]
    group_exp = jnp.sum(
        hot[0] * exp_scores[:, 0:1] + hot[1] * exp_scores[:, 1:2], axis=0, keepdims=True
    )
    group_weight = jnp.sum(hot[0] * weight[0] + hot[1] * weight[1], axis=0, keepdims=True)
    own_row = lax.broadcasted_iota(jnp.int32, (slabs, 1), 0) == place.seq
    loss = jnp.zeros((1, 1), F32)
    coefs = []
    for j in range(2):
        denom = jnp.sum(hot[j] * group_exp, axis=1, keepdims=True)
        target = weight[j] / jnp.sum(hot[j] * group_weight, axis=1, keepdims=True)
        score = squashed[:, j : j + 1]
        loss = loss + jnp.sum(target * (score - jnp.log(denom)), axis=0, keepdims=True)
        tanh_j = tanh_raw[:, j : j + 1]
        grad = (
            GRAD_SCALE
            / slabs
            * (exp_scores[:, j : j + 1] / denom - target)
            * 3.0
            * (1.0 - tanh_j * tanh_j)
        )
        coefs.append(jnp.sum(jnp.where(own_row, grad, 0.0), axis=0, keepdims=True))
    loss_ref[...] = -loss / slabs
    coef = jnp.where(in_second, coefs[1] / len1.astype(F32), coefs[0] / len0.astype(F32))

    for h in range(LOCAL_HEADS):
        cols = slice(h * E, (h + 1) * E)
        out = outs_ref[h]
        sigma = 1.0 / (1.0 + jnp.exp(-out))
        dout = (coef * readout_ref[:, cols] * sigma * (1.0 + out * (1.0 - sigma))).astype(BF)
        dout_ref[h] = dout
        zero = jnp.zeros_like(dout)
        split = jnp.concatenate(
            [jnp.where(in_second, zero, dout), jnp.where(in_second, dout, zero)], axis=1
        )
        sums = scaling * dot_tn(q_ref[:, cols], split)
        grads_ref[0, h] = sums[:, :E].astype(BF)
        grads_ref[1, h] = sums[:, E:].astype(BF)

    def backward(h):
        cols = slice(h * E, (h + 1) * E)
        q, k, v = q_ref[:, cols], k_ref[:, cols], v_ref[:, cols]
        dout = dout_ref[h]
        weights = jnp.where(mask_of(width, width), dot_nt(dout, v), 0.0).astype(BF)
        far = jnp.where(in_second, dot_nt(dout, states_ref[1, h]), dot_nt(dout, states_ref[0, h]))
        dq_ref[:, cols] = (scaling * (dot_nn(weights, k) + far)).astype(BF)
        dk_ref[:, cols] = (scaling * dot_tn(weights, q)).astype(BF)
        dv_ref[:, cols] = (scaling * dot_tn(attn_ref[h], dout)).astype(BF)

    def between(at):
        if at < 2:
            backward(at)
        else:
            backward(2)
            backward(3)

    def pick(src, dest, r):
        wanted = meta_ref[dest] + r
        both0 = cand_ref[2 * src] == wanted
        both1 = cand_ref[2 * src + 1] == wanted
        return jnp.where(both0, jnp.where(both1, 2, 0), jnp.where(both1, 1, 3))

    route(place, grads_ref, 2, 3, 4, pick, scratch, between, 2, 3)
    final, swapped = scratch[5], scratch[6]
    last = meta_ref[slabs + place.seq] - meta_ref[place.seq]
    for j in range(PIECES):
        use = jnp.where(last == j, 1.0, 0.0).astype(F32)
        for side, rows in ((place.core, final[place.core, j]), (1 - place.core, swapped[j])):
            heads = pl.ds(HALF * side, HALF)
            right_ref[j, heads] = (
                rows.astype(F32) + use * states_ref[3, heads].astype(F32)
            ).astype(BF)


def prompt_kernel(
    meta_ref,
    ends_ref,
    q_ref,
    k_ref,
    v_ref,
    g_ref,
    states_ref,
    right_ref,
    dq_ref,
    dk_ref,
    dv_ref,
    dk_acc,
    dv_acc,
):
    width = q_ref.shape[0]
    slab = lax.axis_index("seq")
    scaling = 1.0 / math.sqrt(E * width)
    end0, end1 = local_ends(meta_ref, ends_ref, slab, width, PIECES)

    def segment_of(spot):
        return (spot >= end0).astype(jnp.int32) + (spot >= end1).astype(jnp.int32)

    dk_acc[...] = jnp.zeros_like(dk_acc)
    dv_acc[...] = jnp.zeros_like(dv_acc)
    carry = states_ref[2, 0]
    for at in range(width // CHUNK):
        rows = slice(at * CHUNK, (at + 1) * CHUNK)
        span = (at + 1) * CHUNK
        i = lax.broadcasted_iota(jnp.int32, (CHUNK, 1), 0) + at * CHUNK
        j = lax.broadcasted_iota(jnp.int32, (1, span), 1)
        same = jnp.logical_and(segment_of(i) == segment_of(j), j <= i)
        q, g = q_ref[rows], g_ref[rows]
        attn = jnp.where(same, dot_nt(q, k_ref[:span]), 0.0).astype(BF)
        weights = jnp.where(same, dot_nt(g, v_ref[:span]), 0.0).astype(BF)
        far = jnp.where(i < end0, dot_nt(g, carry), 0.0)
        dq_ref[rows] = (scaling * (dot_nn(weights, k_ref[:span]) + far)).astype(BF)
        dk_acc[:span] += dot_tn(weights, q)
        dv_acc[:span] += dot_tn(attn, g)
    spot = lax.broadcasted_iota(jnp.int32, (width, 1), 0)
    segment = segment_of(spot)
    dk = scaling * dk_acc[...]
    dv = scaling * dv_acc[...]
    for j in range(PIECES):
        here = segment == j
        zero = jnp.zeros_like(v_ref[...])
        dk = dk + dot_nt(jnp.where(here, v_ref[...], zero), right_ref[j, 0])
        dv = dv + dot_nn(jnp.where(here, k_ref[...], zero), right_ref[j, 0])
    dk_ref[...] = dk.astype(BF)
    dv_ref[...] = dv.astype(BF)


def per_device(
    prompt_q,
    prompt_k,
    prompt_v,
    prompt_grad,
    cand_q,
    cand_k,
    cand_v,
    readout,
    prompt_ends,
    cand_lengths,
    cand_prompt,
    cand_ranks,
):
    slabs = lax.axis_size("seq")
    width = prompt_q.shape[0]
    cand_width = cand_q.shape[0]
    flat = prompt_q.shape[1]
    starts = jnp.arange(slabs, dtype=jnp.int32) * width
    marks = jnp.concatenate([starts, starts + (width - 1)])
    meta = jnp.sum((prompt_ends[None, :] <= marks[:, None]).astype(jnp.int32), axis=1)
    table = jnp.concatenate(
        [cand_prompt.reshape(slabs, 2), cand_ranks.reshape(slabs, 2)], axis=1
    )
    head_block = pl.BlockSpec((width, E), lambda h: (0, h))

    rows = pl.pallas_call(
        pieces_kernel,
        grid=(LOCAL_HEADS,),
        out_shape=jax.ShapeDtypeStruct((4, LOCAL_HEADS, E, E), BF),
        in_specs=[SMEM_SPEC, SMEM_SPEC, head_block, head_block, head_block, head_block],
        out_specs=pl.BlockSpec((4, 1, E, E), lambda h: (0, h, 0, 0)),
        name="pieces",
    )(meta, prompt_ends, prompt_q, prompt_k, prompt_v, prompt_grad)

    states = pl.pallas_call(
        forward_kernel,
        out_shape=jax.ShapeDtypeStruct((4, LOCAL_HEADS, E, E), BF),
        in_specs=[SMEM_SPEC, SMEM_SPEC, VMEM_SPEC],
        out_specs=VMEM_SPEC,
        scratch_shapes=route_scratch(5, 4),
        compiler_params=pltpu.CompilerParams(
            collective_id=0, has_side_effects=True, vmem_limit_bytes=48 << 20
        ),
        name="route_states",
    )(meta, cand_prompt, rows)

    cand_shape = jax.ShapeDtypeStruct((cand_width, flat), BF)
    cand_dq, cand_dk, cand_dv, right, loss = pl.pallas_call(
        cand_kernel,
        out_shape=(
            cand_shape,
            cand_shape,
            cand_shape,
            jax.ShapeDtypeStruct((PIECES, LOCAL_HEADS, E, E), BF),
            jax.ShapeDtypeStruct((1, 1), F32),
        ),
        in_specs=[SMEM_SPEC, SMEM_SPEC, SMEM_SPEC] + [VMEM_SPEC] * 6,
        out_specs=[VMEM_SPEC] * 5,
        scratch_shapes=[
            pltpu.VMEM((LOCAL_HEADS, cand_width, cand_width), BF),
            pltpu.VMEM((LOCAL_HEADS, cand_width, E), F32),
            pltpu.VMEM((LOCAL_HEADS, cand_width, E), BF),
            pltpu.VMEM((2, LOCAL_HEADS, E, E), BF),
            pltpu.VMEM((1, E), F32),
            pltpu.VMEM((4, 1, E), F32),
            pltpu.VMEM((1, E), F32),
            pltpu.VMEM((slabs, 1, E), F32),
            pltpu.SemaphoreType.DMA((3,)),
            pltpu.SemaphoreType.DMA((3,)),
            pltpu.SemaphoreType.DMA((slabs,)),
            pltpu.SemaphoreType.DMA((slabs,)),
        ]
        + route_scratch(4, 3),
        compiler_params=pltpu.CompilerParams(
            collective_id=1, has_side_effects=True, vmem_limit_bytes=48 << 20
        ),
        name="candidates",
    )(
        meta,
        cand_prompt,
        cand_lengths,
        states,
        cand_q,
        cand_k,
        cand_v,
        readout.reshape(1, flat),
        table,
    )

    row_block = lambda rows: pl.BlockSpec((rows, 1, E, E), lambda h: (0, h, 0, 0))
    prompt_shape = jax.ShapeDtypeStruct((width, flat), BF)
    prompt_dq, prompt_dk, prompt_dv = pl.pallas_call(
        prompt_kernel,
        grid=(LOCAL_HEADS,),
        out_shape=(prompt_shape,) * 3,
        in_specs=[
            SMEM_SPEC,
            SMEM_SPEC,
            head_block,
            head_block,
            head_block,
            head_block,
            row_block(4),
            row_block(PIECES),
        ],
        out_specs=(head_block,) * 3,
        scratch_shapes=[pltpu.VMEM((width, E), F32)] * 2,
        name="prompt_backward",
    )(meta, prompt_ends, prompt_q, prompt_k, prompt_v, prompt_grad, states, right)

    return (
        prompt_dq,
        prompt_dk,
        prompt_dv,
        cand_dq,
        cand_dk,
        cand_dv,
        loss.reshape(()),
    )


def solution(mesh):
    both = P("seq", "head")
    return jax.shard_map(
        per_device,
        mesh=mesh,
        in_specs=(
            both,
            both,
            both,
            both,
            both,
            both,
            both,
            P("head"),
            P(),
            P("seq", None),
            P(),
            P(),
        ),
        out_specs=(both, both, both, both, both, both, P()),
        check_vma=False,
    )
```

time: 636 us -> 99.3 us (0.16)
  waiting for transfers between devices: 296 us -> 0 us
  blocking collectives: 130 us -> 0 us
  Pallas kernels: 0 us -> 90.1 us
  matrix products: 57.8 us -> 0 us
  local copies, waits for them, and re-layouts: 60 us -> 5.55 us
  other arithmetic: 48.1 us -> 0.75 us
  loops' own time: 21.1 us -> 0 us
  between operations: 19.4 us -> 2.53 us
    unnamed x5 -> x0, waiting for transfers between devices: 169 us -> none
    all_gather x3 -> x0, waiting for transfers between devices: 126 us -> none  [the longest x1 118 us: per_device(): lax.all_gather(end_slots.astype(jnp.bfloat16), 'seq', axis=0, tiled=True)]
    pallas_call x0 -> x4, Pallas kernels: none -> 90.1 us  [the longest x1 38.2 us: per_device(): pl.pallas_call(cand_kernel, out_shape=(cand_shape, cand_shape, cand_shape...]
    unnamed x1 -> x0, blocking collectives: 65.7 us -> none
    psum x1 -> x0, blocking collectives: 64.6 us -> none  [per_device(): raw_scores = lax.psum(placed, ('seq', 'head'))]
    dot_general x20 -> x0, matrix products: 57.8 us -> none  [the longest x1 8.15 us: per_device(): jnp.einsum('jr,rhde->jhde', matches, shard_rows, preferred_element_type=j...]
    add x34 -> x0, other arithmetic: 33.2 us -> none  [the longest x31 32.5 us: chain_combine(): later[0] + (1.0 - later[1]) * earlier[0]]
    another operation x2 -> x0, loops' own time: 21.1 us -> none  [prefix(): return lax.fori_loop(0, ahead, one, state)]
  transfers between devices with their start and end apart: 4 -> 0, of which waited for: 3 -> 0; matrix products, arithmetic and copies ran while one was open for 8% -> 0% of each run, Pallas kernels for 0% -> 0%
where the time goes in v1:
time: 99.3 us; the launch traced here: 99 us
  Pallas kernels  90.1 us (91%)
  local copies, waits for them, and re-layouts  5.55 us (6%)
  between operations  2.53 us (3%)
    pallas_call x1, Pallas kernels, per_device(): pl.pallas_call(cand_kernel, out_shape=(cand_shape, cand_shape, cand_shape...  38.2 us
    pallas_call x1, Pallas kernels, per_device(): pl.pallas_call(forward_kernel, out_shape=jax.ShapeDtypeStruct((4, LOCAL_H...  34 us
    pallas_call x1, Pallas kernels, per_device(): pl.pallas_call(prompt_kernel, grid=(LOCAL_HEADS,), out_shape=(prompt_shap...  12.8 us
    unnamed x27, local copies, waits for them, and re-layouts  5.37 us
    pallas_call x1, Pallas kernels, per_device(): pl.pallas_call(pieces_kernel, grid=(LOCAL_HEADS,), out_shape=jax.ShapeDty...  5.14 us

profile of v1, /device:TPU:1, one launch (start us, length us, event | category | flops | bytes accessed | tf_op | source)
XLA Modules:
  0.0 99.0 jit_solution(10309296974799793167)
XLA Ops:
  0.6 0.0 copy-start.10
  0.7 0.1 pad_add_fusion.1
  0.7 0.6 copy-done.10
  1.3 0.0 copy-start.11
  1.3 0.6 convert_reduce_fusion.meta_ref
  1.9 0.1 copy-done.11
  2.0 0.0 copy-start.7
  2.0 0.1 reshape.30
  2.1 0.6 copy-done.7
  2.6 0.1 reshape.29
  2.7 0.1 pad_add_fusion.table_ref
  2.8 0.0 copy-start.6
  2.8 0.0 copy-start.4
  2.8 0.0 copy-start.8
  2.8 5.1 %pieces.1.rows_ref = bf16[4,4,128,128]{3,2,1,0:T(8,128)(2,1)} custom-call(s32[64]{0:T(128)} %convert_reduce_fusion.meta_ref, s32[32]{0:T(128)} %ends_ref.3, bf16[1024,512]{1,0:T(8,128)(2,1)} %q_ref.5, bf16[1024,512]{1,0:T(8,128)(2,1)} %k_ref.5, bf16[1024,512]{1,0:T(8,128)(2,1)} %v_ref.5, bf16[1024,512]{1,0:T(8,128)(2,1)} %g_ref.3), custom_call_target="tpu_custom_call" | custom-call | tf_op jit(solution)/shard_map/pieces/pallas_call | solution.py:561
  7.9 0.0 copy-done.6
  7.9 0.0 copy-start.1
  7.9 1.0 %copy-done.1 = bf16[4,4,128,128]{3,2,1,0:T(8,128)(2,1)S(1)} copy-done((bf16[4,4,128,128]{3,2,1,0:T(8,128)(2,1)S(1)}, bf16[4,4,128,128]{3,2,1,0:T(8,128)(2,1)}, u32[]{:S(2)}) %copy-start.1) | copy-done | bytes 524312
  9.0 0.0 copy-start.2
  9.0 0.0 copy-start.3
  9.0 0.0 copy-start.9
  9.0 34.0 %route_states.1.states_ref = bf16[4,4,128,128]{3,2,1,0:T(8,128)(2,1)S(1)} custom-call(s32[64]{0:T(128)S(1)} %copy-done.6, s32[64]{0:T(128)S(1)} %copy-done.7, bf16[4,4,128,128]{3,2,1,0:T(8,128)(2,1)S(1)} %copy-done.1), custom_call_target="tpu_custom_call" | custom-call | tf_op jit(solution)/shard_map/route_states/pallas_call | solution.py:570
  43.0 0.0 copy-done.4
  43.0 0.0 copy-done.8
  43.0 0.0 copy-done.2
  43.0 0.0 copy-done.3
  43.0 0.0 copy-done.9
  43.0 0.0 copy-start
  43.0 38.2 %candidates.1 = (bf16[512,512]{1,0:T(8,128)(2,1)S(1)}, bf16[512,512]{1,0:T(8,128)(2,1)S(1)}, bf16[512,512]{1,0:T(8,128)(2,1)S(1)}, bf16[3,4,128,128]{3,2,1,0:T(8,128)(2,1)S(1)}, f32[1,1]{1,0:T(1,128)}) custom-call(s32[64]{0:T(128)S(1)} %copy-done.6, s32[64]{0:T(128)S(1)} %copy-done.7, s32[1,2]{1,0:T(1,128)S(1)} %copy-done.9, ...), custom_call_target="tpu_custom_call" | custom-call | tf_op jit(solution)/shard_map/candidates/pallas_call | solution.py:583
  81.3 0.0 copy-done
  81.3 0.0 copy-start.5
  81.3 0.7 copy-done.5
  82.0 12.8 %prompt_backward.1 = (bf16[1024,512]{1,0:T(8,128)(2,1)}, bf16[1024,512]{1,0:T(8,128)(2,1)}, bf16[1024,512]{1,0:T(8,128)(2,1)}) custom-call(s32[64]{0:T(128)} %convert_reduce_fusion.meta_ref, s32[32]{0:T(128)} %ends_ref.3, bf16[1024,512]{1,0:T(8,128)(2,1)} %q_ref.5, bf16[1024,512]{1,0:T(8,128)(2,1)} %k_ref.5, bf16[1024,512]{1,0:T(8,128)(2,1)} %v_ref.5, ...), custom_call_target="tpu_custom_call" | custom-call | tf_op jit(solution)/shard_map/prompt_backward/pallas_call | solution.py:627
  94.8 0.8 copy.26
  95.6 0.8 copy.27
  96.4 0.8 copy.28
  (1 shorter events, 0.0 us)
Async XLA Ops:
  0.6 0.7 copy-start.10
  1.3 0.7 copy-start.11
  2.0 0.7 copy-start.7
  2.8 5.1 %copy-start.6 = (s32[64]{0:T(128)S(1)}, s32[64]{0:T(128)}, u32[]{:S(2)}) copy-start(s32[64]{0:T(128)} %convert_reduce_fusion.meta_ref) | copy-start | bytes 772
  2.8 40.2 %copy-start.4 = (bf16[512,512]{1,0:T(8,128)(2,1)S(1)}, bf16[512,512]{1,0:T(8,128)(2,1)}, u32[]{:S(2)}) copy-start(bf16[512,512]{1,0:T(8,128)(2,1)} %v_ref.4) | copy-start | bytes 1572868
  2.8 40.2 %copy-start.8 = (f32[512]{0:T(512)S(1)}, f32[512]{0:T(512)}, u32[]{:S(2)}) copy-start(f32[512]{0:T(512)} %param.19) | copy-start | bytes 6148
  7.9 1.0 %copy-start.1 = (bf16[4,4,128,128]{3,2,1,0:T(8,128)(2,1)S(1)}, bf16[4,4,128,128]{3,2,1,0:T(8,128)(2,1)}, u32[]{:S(2)}) copy-start(bf16[4,4,128,128]{3,2,1,0:T(8,128)(2,1)} %pieces.1.rows_ref) | copy-start | bytes 1572868
  9.0 34.0 %copy-start.2 = (bf16[512,512]{1,0:T(8,128)(2,1)S(1)}, bf16[512,512]{1,0:T(8,128)(2,1)}, u32[]{:S(2)}) copy-start(bf16[512,512]{1,0:T(8,128)(2,1)} %q_ref.4) | copy-start | bytes 1572868
  9.0 34.0 %copy-start.3 = (bf16[512,512]{1,0:T(8,128)(2,1)S(1)}, bf16[512,512]{1,0:T(8,128)(2,1)}, u32[]{:S(2)}) copy-start(bf16[512,512]{1,0:T(8,128)(2,1)} %k_ref.4) | copy-start | bytes 1572868
  9.0 34.0 %copy-start.9 = (s32[1,2]{1,0:T(1,128)S(1)}, s32[1,2]{1,0:T(1,128)}, u32[]{:S(2)}) copy-start(s32[1,2]{1,0:T(1,128)} %lens_ref.1) | copy-start | bytes 28
  43.0 38.2 %copy-start = (bf16[4,4,128,128]{3,2,1,0:T(8,128)(2,1)}, bf16[4,4,128,128]{3,2,1,0:T(8,128)(2,1)S(1)}, u32[]{:S(2)}) copy-start(bf16[4,4,128,128]{3,2,1,0:T(8,128)(2,1)S(1)} %route_states.1.states_ref) | copy-start | bytes 1572868
  81.3 0.7 copy-start.5

commit v2 on v1

v2 whole, which is shorter than its diff:
```python
import functools
import math

import jax
import jax.numpy as jnp
from jax import lax
from jax.experimental import pallas as pl
from jax.experimental.pallas import tpu as pltpu
from jax.sharding import PartitionSpec as P

E = 128
LOCAL_HEADS = 4
HALF = LOCAL_HEADS // 2
RING = 4
CHUNK = 256
PIECES = 3
CHIP_ROWS = 5
CHIP_ENDS = 4
SUM01, SUM23, NONE = 4, 5, 6
FAR = 1 << 30
GRAD_SCALE = 1048576.0
MESH = pl.DeviceIdType.MESH
BF = jnp.bfloat16
F32 = jnp.float32

VMEM_SPEC = pl.BlockSpec(memory_space=pltpu.VMEM)
SMEM_SPEC = pl.BlockSpec(memory_space=pltpu.SMEM)


def dot_nn(a, b):
    return lax.dot_general(a, b, (((1,), (0,)), ((), ())), preferred_element_type=F32)


def dot_nt(a, b):
    return lax.dot_general(a, b, (((1,), (1,)), ((), ())), preferred_element_type=F32)


def dot_tn(a, b):
    return lax.dot_general(a, b, (((0,), (0,)), ((), ())), preferred_element_type=F32)


def local_ends(meta_ref, ends_ref, slab, width, count):
    first = meta_ref[slab]
    last = ends_ref.shape[0] - 1
    end0 = ends_ref[jnp.minimum(first, last)] - slab * width
    end1 = jnp.where(
        first + 1 <= last, ends_ref[jnp.minimum(first + 1, last)] - slab * width, FAR
    )
    return end0, end1


class Place:
    def __init__(self):
        self.seq = lax.axis_index("seq")
        self.head = lax.axis_index("head")
        self.core = self.seq % 2
        x = (self.seq // 2) % RING
        z = self.seq // (2 * RING)
        self.pos_a = z * (1 - self.core) + x * self.core
        self.pos_b = x * (1 - self.core) + z * self.core
        self.step_a = 8 - 6 * self.core
        self.step_b = 2 + 6 * self.core

    def chip_at(self, move_a, move_b):
        return ((self.pos_a + move_a) % RING) * self.step_a + (
            (self.pos_b + move_b) % RING
        ) * self.step_b

    def neighbour(self, move_a, move_b):
        return (self.chip_at(move_a, move_b) + self.core, self.head)

    def partner(self):
        return (self.seq + 1 - 2 * self.core, self.head)


class Spread:
    COPIES = 6

    @staticmethod
    def scratch(rows, kind):
        return [
            pltpu.VMEM((RING, HALF, rows, E, E), kind),
            pltpu.VMEM((2, rows, E, E), F32),
            pltpu.VMEM((HALF, rows, E, E), kind),
            pltpu.VMEM((2, HALF, rows, E, E), kind),
            pltpu.SemaphoreType.DMA((Spread.COPIES,)),
            pltpu.SemaphoreType.DMA((Spread.COPIES,)),
        ]

    def __init__(self, place, rows, scratch, term):
        self.rows, self.term = rows, term
        self.parts, self.exact, self.passed, self.arrived, send, recv = scratch
        left, right = place.neighbour(0, RING - 1), place.neighbour(0, 1)
        parts, passed, arrived = self.parts, self.passed, self.arrived
        pairs = (
            (parts.at[2, 0], passed.at[0], left),
            (parts.at[2, 1], passed.at[1], right),
            (parts.at[3, 1], arrived.at[0, 1], left),
            (parts.at[1, 0], arrived.at[1, 0], right),
            (parts.at[3, 0], arrived.at[0, 0], left),
            (parts.at[1, 1], arrived.at[1, 1], right),
        )
        self.copies = [
            remote_copy(src, dst, send.at[at], recv.at[at], device)
            for at, (src, dst, device) in enumerate(pairs)
        ]

    def begin(self):
        for at, (m, i) in enumerate(((2, 0), (2, 1), (3, 1), (1, 0))):
            for r in range(self.rows):
                self.parts[m, i, r] = self.term(m, i, r).astype(self.parts.dtype)
            self.copies[at].start()

    def pass_on(self):
        for at, (m, i) in enumerate(((3, 0), (1, 1))):
            for r in range(self.rows):
                self.exact[at, r] = self.term(m, i, r).astype(F32)
        for at, (m, i) in enumerate(((3, 0), (1, 1))):
            self.copies[at].wait_recv()
            for r in range(self.rows):
                self.parts[m, i, r] = (
                    self.exact[at, r] + self.passed[i, r].astype(F32)
                ).astype(self.parts.dtype)
            self.copies[4 + at].start()

    def arrive(self):
        for copy in self.copies[2:]:
            copy.wait_recv()

    def result(self, i, r):
        return (
            self.term(0, i, r).astype(F32)
            + self.arrived[0, i, r].astype(F32)
            + self.arrived[1, i, r].astype(F32)
        )

    def finish(self):
        for copy in self.copies:
            copy.wait_send()


class Gather:
    COPIES = 6

    def __init__(self, place, block, send, recv):
        left, right = place.neighbour(RING - 1, 0), place.neighbour(1, 0)
        pairs = (
            (block(0, 0), block(1, 0), left),
            (block(0, 1), block(3, 1), right),
            (block(0, 1), block(1, 1), left),
            (block(0, 0), block(3, 0), right),
            (block(1, 0), block(2, 0), left),
            (block(3, 1), block(2, 1), right),
        )
        self.copies = [
            remote_copy(src, dst, send.at[at], recv.at[at], device)
            for at, (src, dst, device) in enumerate(pairs)
        ]

    def begin(self):
        for copy in self.copies[:4]:
            copy.start()

    def pass_on(self):
        for at in range(2):
            self.copies[at].wait_recv()
            self.copies[4 + at].start()

    def arrive(self):
        for copy in self.copies[2:]:
            copy.wait_recv()
        for copy in self.copies:
            copy.wait_send()


def remote_copy(src, dst, send, recv, device):
    return pltpu.make_async_remote_copy(
        src_ref=src,
        dst_ref=dst,
        send_sem=send,
        recv_sem=recv,
        device_id=device,
        device_id_type=MESH,
    )


def flag(condition):
    return jnp.where(condition, 1.0, 0.0).astype(F32)


def lanes(head):
    return pl.ds(pl.multiple_of(head * E, E), E)


def main_kernel(
    meta_ref,
    ends_ref,
    cand_ref,
    lens_ref,
    ranks_ref,
    readout_ref,
    pq_hbm,
    pk_hbm,
    pv_hbm,
    pg_hbm,
    cq_hbm,
    ck_hbm,
    cv_hbm,
    dq_hbm,
    dkp_hbm,
    dvp_hbm,
    cdq_hbm,
    cdk_hbm,
    cdv_hbm,
    right_ref,
    loss_ref,
    pq,
    pk,
    pv,
    pg,
    cq,
    ck,
    cv,
    masks,
    dq_acc,
    dkp,
    dvp,
    dq_out,
    cdq,
    cdk,
    cdv,
    own,
    theirs,
    mail,
    qg_own,
    qg_theirs,
    qg_mail,
    states,
    states_mail,
    states_in,
    carry_mail,
    carry_in,
    carry,
    chip_carry,
    right_sum,
    right_mail,
    right_in,
    attn_ref,
    outs_ref,
    dout_ref,
    grads_mail,
    mine_ref,
    heads_ref,
    total_ref,
    scores_ref,
    gathered,
    gathered_wide,
    gathered_qg,
    gathered_grads,
    table_ref,
    in_sem,
    out_sem,
    swap_send,
    swap_recv,
    ring_send,
    ring_recv,
    y_send,
    y_recv,
    s_send,
    s_recv,
    *spread_scratch,
):
    place = Place()
    core = place.core
    slabs = meta_ref.shape[0] // 2
    planes = lax.axis_size("head")
    width = pq.shape[0]
    cand_width = cq.shape[0]
    scaling = 1.0 / math.sqrt(E * width)
    barrier = pltpu.get_barrier_semaphore()

    def other_slab(at):
        return (place.seq + at) % slabs, place.head

    def hello(at, held):
        pl.semaphore_signal(barrier, inc=1, device_id=other_slab(at), device_id_type=MESH)
        return held

    loads = [
        pltpu.make_async_copy(src, dst, in_sem.at[at])
        for at, (src, dst) in enumerate(
            (
                (pk_hbm, pk),
                (pv_hbm, pv),
                (pg_hbm, pg),
                (pq_hbm, pq),
                (cq_hbm, cq),
                (ck_hbm, ck),
                (cv_hbm, cv),
            )
        )
    ]
    loads[0].start()
    loads[1].start()
    lax.fori_loop(1, slabs, hello, 0)
    planes_other = [(place.seq, (place.head + at) % planes) for at in range(1, planes)]
    for device in planes_other:
        pl.semaphore_signal(barrier, inc=1, device_id=device, device_id_type=MESH)

    def store(at, src, dst):
        copy = pltpu.make_async_copy(src, dst, out_sem.at[at])
        copy.start()
        return copy

    def swap(at, src, dst):
        return remote_copy(src, dst, swap_send.at[at], swap_recv.at[at], place.partner())

    end0, end1 = local_ends(meta_ref, ends_ref, place.seq, width, PIECES)
    spot = lax.broadcasted_iota(jnp.int32, (width, E), 0)
    masks[0] = flag(spot < end0).astype(BF)
    masks[1] = flag(jnp.logical_and(spot >= end0, spot < end1)).astype(BF)
    masks[2] = flag(spot >= end1).astype(BF)

    def piece_sums(head):
        v = pv[:, lanes(head)]
        split = jnp.concatenate([v * masks[j] for j in range(PIECES)], axis=1)
        return dot_tn(pk[:, lanes(head)], split)

    loads[0].wait()
    loads[1].wait()
    for load in loads[2:]:
        load.start()
    pieces_swaps = []
    for i in range(HALF):
        sums = piece_sums(HALF * (1 - core) + i)
        for j in range(PIECES):
            mail[i, j] = sums[:, j * E : (j + 1) * E]
        if i == 0:
            pl.semaphore_wait(barrier, slabs - 1 + planes - 1)
        pieces_swaps.append(swap(6 * i, mail.at[i], theirs.at[i, pl.ds(0, PIECES)]))
        pieces_swaps[-1].start()
    for i in range(HALF):
        sums = piece_sums(HALF * core + i)
        for j in range(PIECES):
            own[j, i] = sums[:, j * E : (j + 1) * E]
        own[PIECES, i] = jnp.zeros((E, E), F32)
        theirs[i, PIECES] = jnp.zeros((E, E), F32)
        for k in range(RING):
            gathered[k, i, CHIP_ENDS - 1] = jnp.zeros((E, E), BF)
            gathered_wide[k, i, 2] = jnp.zeros((E, E), F32)
            gathered_grads[k, i, NONE] = jnp.zeros((E, E), BF)

    chip = place.chip_at(0, 0)
    first0, first1 = meta_ref[chip], meta_ref[chip + 1]
    last0, last1 = meta_ref[slabs + chip], meta_ref[slabs + chip + 1]
    off = jnp.clip(first1 - first0, 0, PIECES - 1)
    off_own, off_theirs = off * core, off * (1 - core)

    def slot_in(j, count):
        return jnp.where(jnp.logical_and(j >= 0, j < count), j, count)

    def chip_row(i, j):
        at_own, at_theirs = slot_in(j - off_own, PIECES), slot_in(j - off_theirs, PIECES)
        return own[at_own, i] + theirs[i, at_theirs]

    tail0 = jnp.where(last0 == last1, slot_in(last0 - first0, PIECES), PIECES)
    tail1 = slot_in(last1 - first1, PIECES)
    tail_own = jnp.where(core == 0, tail0, tail1)
    tail_theirs = jnp.where(core == 0, tail1, tail0)
    wide_ring = Gather(
        place,
        lambda k, i: gathered_wide.at[k, i, pl.ds(0, 2)],
        ring_send.at[0],
        ring_recv.at[0],
    )
    ends_ring = Gather(
        place,
        lambda k, i: gathered.at[k, i, pl.ds(0, CHIP_ENDS - 1)],
        ring_send.at[1],
        ring_recv.at[1],
    )
    for copy in pieces_swaps:
        copy.wait()
    for i in range(HALF):
        gathered_wide[0, i, 0] = chip_row(i, 0)
        gathered_wide[0, i, 1] = own[tail_own, i] + theirs[i, tail_theirs]
    wide_ring.begin()
    for i in range(HALF):
        for j in range(1, CHIP_ENDS):
            gathered[0, i, j - 1] = chip_row(i, j).astype(BF)
    ends_ring.begin()

    def segment_of(at):
        return (at >= end0).astype(jnp.int32) + (at >= end1).astype(jnp.int32)

    def prompt_task(at, low, high):
        rows = slice(at * CHUNK, (at + 1) * CHUNK)
        span = (at + 1) * CHUNK
        i = lax.broadcasted_iota(jnp.int32, (CHUNK, 1), 0) + at * CHUNK
        j = lax.broadcasted_iota(jnp.int32, (1, span), 1)
        same = jnp.logical_and(segment_of(i) == segment_of(j), j <= i)

        def one(h, held):
            cols = lanes(h)
            q, g = pq[rows, cols], pg[rows, cols]
            attn = jnp.where(same, dot_nt(q, pk[:span, cols]), 0.0).astype(BF)
            weights = jnp.where(same, dot_nt(g, pv[:span, cols]), 0.0).astype(BF)
            dq_acc[rows, cols] = dot_nn(weights, pk[:span, cols])
            dk = scaling * dot_tn(weights, q)
            dv = scaling * dot_tn(attn, g)
            if span == width:
                dkp[:, cols] = dk
                dvp[:, cols] = dv
            else:
                dkp[:span, cols] += dk
                dvp[:span, cols] += dv
            return held

        lax.fori_loop(low, high, one, 0)

    len0 = lens_ref[0, 0]
    len1 = lens_ref[0, 1]
    in_second = lax.broadcasted_iota(jnp.int32, (cand_width, 1), 0) >= len0

    def same_cand():
        i = lax.broadcasted_iota(jnp.int32, (cand_width, 1), 0)
        j = lax.broadcasted_iota(jnp.int32, (1, cand_width), 1)
        return jnp.logical_and(j <= i, (i >= len0).astype(jnp.int32) == (j >= len0).astype(jnp.int32))

    def cand_near(low, high):
        if low == 0:
            for load in loads[4:]:
                load.wait()

        def one(h, held):
            cols = lanes(h)
            attn = jnp.where(same_cand(), dot_nt(cq[:, cols], ck[:, cols]), 0.0).astype(BF)
            attn_ref[h] = attn
            outs_ref[h] = dot_nn(attn, cv[:, cols])
            return held

        lax.fori_loop(low, high, one, 0)

    def cand_backward(low, high):
        def one(h, held):
            cols = lanes(h)
            dout = dout_ref[h]
            weights = jnp.where(same_cand(), dot_nt(dout, cv[:, cols]), 0.0).astype(BF)
            far = jnp.where(in_second, dot_nt(dout, states[1, h]), dot_nt(dout, states[0, h]))
            cdq[:, cols] = (scaling * (dot_nn(weights, ck[:, cols]) + far)).astype(BF)
            cdk[:, cols] = (scaling * dot_tn(weights, cq[:, cols])).astype(BF)
            cdv[:, cols] = (scaling * dot_tn(attn_ref[h], dout)).astype(BF)
            return held

        lax.fori_loop(low, high, one, 0)

    def dq_finish():
        def one(h, held):
            cols = lanes(h)
            far = dot_nt(pg[:, cols], carry[h])
            inside = lax.broadcasted_iota(jnp.int32, (width, 1), 0) < end0
            dq_out[:, cols] = (scaling * (dq_acc[:, cols] + jnp.where(inside, far, 0.0))).astype(BF)
            return held

        lax.fori_loop(0, LOCAL_HEADS, one, 0)

    loads[2].wait()
    loads[3].wait()

    def qg_sum(head):
        return scaling * dot_tn(pq[:, lanes(head)], pg[:, lanes(head)] * masks[0])

    for i in range(HALF):
        qg_mail[i] = qg_sum(HALF * (1 - core) + i)
    qg_swap = swap(1, qg_mail, qg_theirs)
    qg_swap.start()
    for i in range(HALF):
        qg_own[i] = qg_sum(HALF * core + i)
    wide_ring.pass_on()
    ends_ring.pass_on()
    prompt_task(3, 0, 3)
    whole = flag(off == 0)

    def carry_term(m, i):
        dest = place.chip_at(0, m)
        total = None
        for k in range(RING):
            src = place.chip_at(k, 0)
            same = jnp.logical_and(meta_ref[slabs + src + 1] == meta_ref[dest], src < dest)
            term = gathered_wide[k, i, jnp.where(same, 1, 2)]
            total = term if total is None else total + term
        return total

    def memory_term(m, i, r):
        if r == 0:
            return carry_term(m, i)
        dest = place.chip_at(0, m)
        total = None
        for k in range(RING):
            src = place.chip_at(k, 0)
            same = jnp.logical_and(meta_ref[src] == meta_ref[slabs + dest + 1], src > dest)
            term = flag(same) * gathered_qg[k, i]
            total = term if total is None else total + term
        return total

    def state_term(m, i, r):
        wanted = cand_ref[2 * place.chip_at(0, m) + r]
        source = jnp.clip((ends_ref[wanted] - 1) // (2 * width), 0, slabs // 2 - 1)
        src_z, src_x = source // RING, source % RING
        src_a = jnp.where(core == 0, src_z, src_x)
        src_b = jnp.where(core == 0, src_x, src_z)
        k_end = (src_a - place.pos_a + RING) % RING
        row = wanted - meta_ref[2 * source]
        inner = jnp.logical_and(src_b == place.pos_b, row > 0)
        total = gathered[k_end, i, jnp.where(inner, jnp.minimum(row - 1, CHIP_ENDS - 2), CHIP_ENDS - 1)].astype(F32)
        for k in range(RING):
            src = place.chip_at(k, 0)
            opens = jnp.logical_and(src < 2 * source, meta_ref[slabs + src + 1] == wanted)
            ends = jnp.logical_and(src == 2 * source, row == 0)
            total = total + gathered_wide[k, i, jnp.where(opens, 1, jnp.where(ends, 0, 2))]
        return total

    def grad_term(m, i, r):
        wanted = meta_ref[place.chip_at(0, m)] + r
        total = None
        for k in range(RING):
            src = 2 * place.chip_at(k, 0)
            is0, is1, is2, is3 = [cand_ref[src + c] == wanted for c in range(4)]
            slot0 = jnp.where(is0, jnp.where(is1, SUM01, 0), jnp.where(is1, 1, NONE))
            slot1 = jnp.where(is2, jnp.where(is3, SUM23, 2), jnp.where(is3, 3, NONE))
            term = gathered_grads[k, i, slot0].astype(F32) + gathered_grads[k, i, slot1].astype(F32)
            total = term if total is None else total + term
        return total

    to_states = Spread(place, 4, spread_scratch[:6], state_term)
    to_memory = Spread(place, 2, spread_scratch[6:12], memory_term)
    to_grads = Spread(place, CHIP_ROWS, spread_scratch[12:], grad_term)

    qg_swap.wait()
    own_scale = jnp.where(core == 0, 1.0, whole)
    their_scale = jnp.where(core == 0, whole, 1.0)
    for i in range(HALF):
        gathered_qg[0, i] = own_scale * qg_own[i] + their_scale * qg_theirs[i]
    wide_ring.arrive()
    ends_ring.arrive()
    to_states.begin()
    cand_near(0, 2)
    to_states.pass_on()
    qg_ring = Gather(place, lambda k, i: gathered_qg.at[k, i], ring_send.at[2], ring_recv.at[2])
    qg_ring.begin()
    cand_near(2, 4)
    qg_ring.pass_on()
    prompt_task(3, 3, 4)
    to_states.arrive()
    for i in range(HALF):
        for r in range(2):
            states_mail[i, r] = to_states.result(i, 2 * (1 - core) + r).astype(BF)
    states_swap = swap(2, states_mail, states_in)
    states_swap.start()
    for i in range(HALF):
        for r in range(2):
            states[r, HALF * core + i] = to_states.result(i, 2 * core + r).astype(BF)
    qg_ring.arrive()
    to_memory.begin()
    states_swap.wait()
    for i in range(HALF):
        for r in range(2):
            states[r, HALF * (1 - core) + i] = states_in[i, r]

    sum_all = jnp.zeros((1, E), F32)
    sum_second = jnp.zeros((1, E), F32)
    for h in range(LOCAL_HEADS):
        cols = slice(h * E, (h + 1) * E)
        far = jnp.where(
            in_second, dot_nn(cq[:, cols], states[1, h]), dot_nn(cq[:, cols], states[0, h])
        )
        out = scaling * (outs_ref[h] + far)
        outs_ref[h] = out
        part = out / (1.0 + jnp.exp(-out)) * readout_ref[:, cols]
        sum_all = sum_all + jnp.sum(part, axis=0, keepdims=True)
        sum_second = sum_second + jnp.sum(jnp.where(in_second, part, 0.0), axis=0, keepdims=True)
    second = jnp.sum(sum_second, axis=1, keepdims=True)
    first = jnp.sum(sum_all - sum_second, axis=1, keepdims=True)
    lane = lax.broadcasted_iota(jnp.int32, (1, E), 1)
    mine_ref[...] = jnp.where(
        lane == 0,
        first / len0.astype(F32),
        jnp.where(lane == 1, second / len1.astype(F32), 0.0),
    )
    to_planes = [
        remote_copy(mine_ref, heads_ref.at[place.head], y_send.at[at], y_recv.at[at], device)
        for at, device in enumerate(planes_other)
    ]
    for copy in to_planes:
        copy.start()
    heads_ref[place.head] = mine_ref[...]
    to_memory.pass_on()
    for copy in to_planes:
        copy.wait()
    total = heads_ref[0]
    for at in range(1, planes):
        total = total + heads_ref[at]
    total_ref[...] = total

    def score_copy(at):
        return remote_copy(
            total_ref, scores_ref.at[place.seq], s_send.at[at], s_recv.at[at], other_slab(at)
        )

    def tell(at, held):
        score_copy(at).start()
        return held

    def told(at, held):
        score_copy(at).wait()
        return held

    def build_table():
        rows = lax.broadcasted_iota(jnp.int32, (slabs, E), 0)

        def one(at, held):
            here = rows == at
            values = (
                cand_ref[2 * at],
                cand_ref[2 * at + 1],
                ranks_ref[2 * at],
                ranks_ref[2 * at + 1],
            )
            return tuple(jnp.where(here, value, old) for value, old in zip(values, held))

        blank = jnp.zeros((slabs, E), jnp.int32)
        for at, plane in enumerate(lax.fori_loop(0, slabs, one, (blank,) * 4)):
            table_ref[at] = plane

    lax.fori_loop(1, slabs, tell, 0)
    scores_ref[place.seq] = total
    build_table()
    prompt_task(2, 0, 3)
    lax.fori_loop(1, slabs, told, 0)

    raw = scores_ref[...].reshape(slabs, E)
    prompts = lax.broadcasted_iota(jnp.int32, (slabs, E), 1)
    tanh_raw = jnp.tanh(raw)
    squashed = 3.0 * tanh_raw
    exp_scores = jnp.exp(squashed)
    hot = [(table_ref[j] == prompts).astype(F32) for j in range(2)]
    weight = [jnp.exp(-table_ref[2 + j].astype(F32)) for j in range(2)]
    group_exp = jnp.sum(
        hot[0] * exp_scores[:, 0:1] + hot[1] * exp_scores[:, 1:2], axis=0, keepdims=True
    )
    group_weight = jnp.sum(hot[0] * weight[0] + hot[1] * weight[1], axis=0, keepdims=True)
    own_row = lax.broadcasted_iota(jnp.int32, (slabs, 1), 0) == place.seq
    loss = jnp.zeros((1, 1), F32)
    coefs = []
    for j in range(2):
        denom = jnp.sum(hot[j] * group_exp, axis=1, keepdims=True)
        target = weight[j][:, 0:1] / jnp.sum(hot[j] * group_weight, axis=1, keepdims=True)
        score = squashed[:, j : j + 1]
        loss = loss + jnp.sum(target * (score - jnp.log(denom)), axis=0, keepdims=True)
        tanh_j = tanh_raw[:, j : j + 1]
        grad = (
            GRAD_SCALE
            / slabs
            * (exp_scores[:, j : j + 1] / denom - target)
            * 3.0
            * (1.0 - tanh_j * tanh_j)
        )
        coefs.append(jnp.sum(jnp.where(own_row, grad, 0.0), axis=0, keepdims=True))
    loss_ref[...] = -loss / slabs
    coef = jnp.where(in_second, coefs[1] / len1.astype(F32), coefs[0] / len0.astype(F32))

    def grad_sums(h):
        out = outs_ref[h]
        sigma = 1.0 / (1.0 + jnp.exp(-out))
        slope = coef * readout_ref[:, lanes(h)] * sigma * (1.0 + out * (1.0 - sigma))
        dout_ref[h] = slope.astype(BF)
        split = jnp.concatenate(
            [
                jnp.where(in_second, 0.0, slope).astype(BF),
                jnp.where(in_second, slope, 0.0).astype(BF),
            ],
            axis=1,
        )
        return scaling * dot_tn(cq[:, lanes(h)], split)

    for i in range(HALF):
        sums = grad_sums(HALF * (1 - core) + i)
        for r in range(2):
            grads_mail[i, r] = sums[:, r * E : (r + 1) * E].astype(BF)
    own_slots = pl.ds(2 * core, 2)
    grads_swap = swap(3, grads_mail, gathered_grads.at[0, :, own_slots])
    grads_swap.start()
    for i in range(HALF):
        sums = grad_sums(HALF * core + i)
        for r in range(2):
            gathered_grads[0, i, 2 * core + r] = sums[:, r * E : (r + 1) * E].astype(BF)
    grads_swap.wait()
    grads_ring = Gather(
        place,
        lambda k, i: gathered_grads.at[k, i, pl.ds(0, 4)],
        ring_send.at[3],
        ring_recv.at[3],
    )
    grads_ring.begin()

    to_memory.arrive()
    seam = slot_in(off, PIECES)

    def carry_row(i, at_core):
        before = jnp.where(core == 0, own[seam, i], theirs[i, seam])
        is_second = flag(at_core == 1)
        keep = jnp.where(at_core == 0, 1.0, whole)
        return (keep * chip_carry[i] + is_second * before).astype(BF)

    for i in range(HALF):
        chip_carry[i] = to_memory.result(i, 0)
        carry_mail[i] = carry_row(i, 1 - core)
    carry_swap = swap(4, carry_mail, carry_in)
    carry_swap.start()
    for i in range(HALF):
        carry[HALF * core + i] = carry_row(i, core)
    cand_backward(0, 2)
    grads_ring.pass_on()
    cand_backward(2, 4)
    outputs = [store(0, cdq, cdq_hbm), store(1, cdk, cdk_hbm), store(2, cdv, cdv_hbm)]
    carry_swap.wait()
    for i in range(HALF):
        carry[HALF * (1 - core) + i] = carry_in[i]
    grads_ring.arrive()
    for k in range(RING):
        for i in range(HALF):
            for target, source in ((SUM01, 0), (SUM23, 2)):
                gathered_grads[k, i, target] = (
                    gathered_grads[k, i, source].astype(F32)
                    + gathered_grads[k, i, source + 1].astype(F32)
                ).astype(BF)
    to_grads.begin()
    to_grads.pass_on()
    prompt_task(2, 3, 4)
    prompt_task(1, 0, 4)
    prompt_task(0, 0, 4)
    outputs += [store(3, dkp, dkp_hbm), store(4, dvp, dvp_hbm)]
    dq_finish()
    outputs.append(store(5, dq_out, dq_hbm))
    to_grads.arrive()
    for i in range(HALF):
        for r in range(CHIP_ROWS):
            right_sum[r, i] = to_grads.result(i, r)

    def later_row(i, at_core):
        chip_later = to_memory.result(i, 1)
        second_qg = jnp.where(core == 0, qg_theirs[i], qg_own[i])
        inner = flag(first1 == last0) * second_qg + flag(last1 == last0) * chip_later
        return jnp.where(at_core == 0, inner, chip_later)

    def right_row(i, j, at_core, later):
        into = jnp.where(at_core == 0, last0 - first0, last1 - first1)
        return (right_sum[j + off * at_core, i] + flag(into == j) * later).astype(BF)

    for i in range(HALF):
        later = later_row(i, 1 - core)
        for j in range(PIECES):
            right_mail[j, i] = right_row(i, j, 1 - core, later)
    right_swap = swap(5, right_mail, right_in)
    right_swap.start()
    for i in range(HALF):
        later = later_row(i, core)
        for j in range(PIECES):
            right_ref[j, HALF * core + i] = right_row(i, j, core, later)
    for spread in (to_states, to_memory, to_grads):
        spread.finish()
    right_swap.wait()
    for i in range(HALF):
        for j in range(PIECES):
            right_ref[j, HALF * (1 - core) + i] = right_in[j, i]
    for copy in outputs:
        copy.wait()


def last_kernel(
    meta_ref,
    ends_ref,
    k_ref,
    v_ref,
    dkp_ref,
    dvp_ref,
    right_ref,
    dq_in,
    cdq_in,
    cdk_in,
    cdv_in,
    dq_ref,
    dk_ref,
    dv_ref,
    cdq_ref,
    cdk_ref,
    cdv_ref,
):
    width = k_ref.shape[0]
    slab = lax.axis_index("seq")
    end0, end1 = local_ends(meta_ref, ends_ref, slab, width, PIECES)
    spot = lax.broadcasted_iota(jnp.int32, (width, 1), 0)
    k, v = k_ref[...], v_ref[...]
    dk = [dot_nt(v, right_ref[j, 0]) for j in range(PIECES)]
    dv = [dot_nn(k, right_ref[j, 0]) for j in range(PIECES)]
    for out, part, far in ((dk_ref, dkp_ref, dk), (dv_ref, dvp_ref, dv)):
        chosen = jnp.where(spot < end0, far[0], jnp.where(spot < end1, far[1], far[2]))
        out[...] = (part[...] + chosen).astype(BF)
    dq_ref[...] = dq_in[...]
    cdq_ref[...] = cdq_in[...]
    cdk_ref[...] = cdk_in[...]
    cdv_ref[...] = cdv_in[...]


def per_device(
    prompt_q,
    prompt_k,
    prompt_v,
    prompt_grad,
    cand_q,
    cand_k,
    cand_v,
    readout,
    prompt_ends,
    cand_lengths,
    cand_prompt,
    cand_ranks,
):
    slabs = lax.axis_size("seq")
    width = prompt_q.shape[0]
    cand_width = cand_q.shape[0]
    flat = prompt_q.shape[1]
    starts = jnp.arange(slabs, dtype=jnp.int32) * width
    marks = jnp.concatenate([starts, starts + (width - 1)])
    meta = jnp.sum((prompt_ends[None, :] <= marks[:, None]).astype(jnp.int32), axis=1)
    any_spec = pl.BlockSpec(memory_space=pl.ANY)
    prompt_shape = jax.ShapeDtypeStruct((width, flat), BF)
    prompt_wide = jax.ShapeDtypeStruct((width, flat), F32)
    cand_shape = jax.ShapeDtypeStruct((cand_width, flat), BF)
    prompt_buf = pltpu.VMEM((width, flat), BF)
    prompt_acc = pltpu.VMEM((width, flat), F32)
    cand_buf = pltpu.VMEM((cand_width, flat), BF)
    half_rows = lambda *lead, kind=BF: pltpu.VMEM(lead + (E, E), kind)
    dma = pltpu.SemaphoreType.DMA
    dq_part, dk_part, dv_part, cand_dq, cand_dk, cand_dv, right, loss = pl.pallas_call(
        main_kernel,
        out_shape=(
            prompt_shape,
            prompt_wide,
            prompt_wide,
            cand_shape,
            cand_shape,
            cand_shape,
            jax.ShapeDtypeStruct((PIECES, LOCAL_HEADS, E, E), BF),
            jax.ShapeDtypeStruct((1, 1), F32),
        ),
        in_specs=[SMEM_SPEC] * 5 + [VMEM_SPEC] + [any_spec] * 7,
        out_specs=[any_spec] * 6 + [VMEM_SPEC] * 2,
        scratch_shapes=[prompt_buf] * 4
        + [cand_buf] * 3
        + [pltpu.VMEM((PIECES, width, E), BF)]
        + [prompt_acc] * 3
        + [prompt_buf]
        + [cand_buf] * 3
        + [
            half_rows(PIECES + 1, HALF, kind=F32),
            half_rows(HALF, PIECES + 1, kind=F32),
            half_rows(HALF, PIECES, kind=F32),
            half_rows(HALF, kind=F32),
            half_rows(HALF, kind=F32),
            half_rows(HALF, kind=F32),
            half_rows(2, LOCAL_HEADS),
            half_rows(HALF, 2),
            half_rows(HALF, 2),
            half_rows(HALF),
            half_rows(HALF),
            half_rows(LOCAL_HEADS),
            half_rows(HALF, kind=F32),
            half_rows(CHIP_ROWS, HALF, kind=F32),
            half_rows(PIECES, HALF),
            half_rows(PIECES, HALF),
            pltpu.VMEM((LOCAL_HEADS, cand_width, cand_width), BF),
            pltpu.VMEM((LOCAL_HEADS, cand_width, E), F32),
            pltpu.VMEM((LOCAL_HEADS, cand_width, E), BF),
            half_rows(HALF, 2),
            pltpu.VMEM((1, E), F32),
            pltpu.VMEM((4, 1, E), F32),
            pltpu.VMEM((1, E), F32),
            pltpu.VMEM((slabs, 1, E), F32),
            half_rows(RING, HALF, CHIP_ENDS),
            half_rows(RING, HALF, 3, kind=F32),
            half_rows(RING, HALF, kind=F32),
            half_rows(RING, HALF, NONE + 1),
            pltpu.VMEM((4, slabs, E), jnp.int32),
            dma((7,)),
            dma((6,)),
            dma((7,)),
            dma((7,)),
            dma((4, 6)),
            dma((4, 6)),
            dma((3,)),
            dma((3,)),
            dma((slabs,)),
            dma((slabs,)),
        ]
        + Spread.scratch(4, F32)
        + Spread.scratch(2, F32)
        + Spread.scratch(CHIP_ROWS, BF),
        compiler_params=pltpu.CompilerParams(
            collective_id=0, has_side_effects=True, vmem_limit_bytes=56 << 20
        ),
        name="exchange",
    )(
        meta,
        prompt_ends,
        cand_prompt,
        cand_lengths,
        cand_ranks,
        readout.reshape(1, flat),
        prompt_q,
        prompt_k,
        prompt_v,
        prompt_grad,
        cand_q,
        cand_k,
        cand_v,
    )

    prompt_block = pl.BlockSpec((width, E), lambda h: (0, h))
    cand_block = pl.BlockSpec((cand_width, E), lambda h: (0, h))
    prompt_dq, prompt_dk, prompt_dv, cand_dq, cand_dk, cand_dv = pl.pallas_call(
        last_kernel,
        grid=(LOCAL_HEADS,),
        out_shape=(prompt_shape,) * 3 + (cand_shape,) * 3,
        in_specs=[SMEM_SPEC] * 2
        + [prompt_block] * 4
        + [pl.BlockSpec((PIECES, 1, E, E), lambda h: (0, h, 0, 0)), prompt_block]
        + [cand_block] * 3,
        out_specs=(prompt_block,) * 3 + (cand_block,) * 3,
        name="finish",
    )(
        meta,
        prompt_ends,
        prompt_k,
        prompt_v,
        dk_part,
        dv_part,
        right,
        dq_part,
        cand_dq,
        cand_dk,
        cand_dv,
    )
    return (
        prompt_dq,
        prompt_dk,
        prompt_dv,
        cand_dq,
        cand_dk,
        cand_dv,
        loss.reshape(()),
    )


def solution(mesh):
    both = P("seq", "head")
    return jax.shard_map(
        per_device,
        mesh=mesh,
        in_specs=(
            both,
            both,
            both,
            both,
            both,
            both,
            both,
            P("head"),
            P(),
            P("seq", None),
            P(),
            P(),
        ),
        out_specs=(both, both, both, both, both, both, P()),
        check_vma=False,
    )
```

time: 99.3 us -> 83.6 us (0.84)
  Pallas kernels: 90.1 us -> 79.6 us
  local copies, waits for them, and re-layouts: 5.55 us -> 0 us
    pallas_call x4 -> x2, Pallas kernels: 90.1 us -> 79.6 us  [the longest x1 72.7 us: per_device(): pl.pallas_call(main_kernel, out_shape=(prompt_shape, prompt_wide, prompt_...]
    unnamed x27 -> x0, local copies, waits for them, and re-layouts: 5.37 us -> none
where the time goes in v2:
time: 83.6 us; the launch traced here: 83.4 us
  Pallas kernels  79.6 us (95%)
  between operations  2.45 us (3%)
  other arithmetic  1.33 us (2%)
    pallas_call x1, Pallas kernels, per_device(): pl.pallas_call(main_kernel, out_shape=(prompt_shape, prompt_wide, prompt_...  72.7 us
    pallas_call x1, Pallas kernels, per_device(): pl.pallas_call(last_kernel, grid=(LOCAL_HEADS,), out_shape=(prompt_shape,...  6.95 us

profile of v2, /device:TPU:1, one launch (start us, length us, event | category | flops | bytes accessed | tf_op | source)
XLA Modules:
  0.0 83.4 jit_solution(7858876194289282313)
XLA Ops:
  0.6 0.1 pad_add_fusion
  0.7 1.3 %convert_reduce_fusion.meta_ref = s32[64]{0:T(128)} fusion(s32[64]{0:T(128)S(1)} %pad_add_fusion, s32[32]{0:T(128)} %ends_ref.3), kind=kLoop, calls=%fused_computation | loop fusion | flops 6080 | bytes 640 | tf_op jit(solution)/shard_map/reduce_sum | solution.py:835
  2.0 72.7 %exchange.1 = (bf16[1024,512]{1,0:T(8,128)(2,1)}, f32[1024,512]{1,0:T(8,128)}, f32[1024,512]{1,0:T(8,128)}, bf16[512,512]{1,0:T(8,128)(2,1)}, bf16[512,512]{1,0:...) custom-call(s32[64]{0:T(128)} %convert_reduce_fusion.meta_ref, ...), custom_call_target="tpu_custom_call" | custom-call | tf_op jit(solution)/shard_map/exchange/pallas_call | solution.py:845
  74.6 7.0 %finish.1 = (bf16[1024,512]{1,0:T(8,128)(2,1)}, bf16[1024,512]{1,0:T(8,128)(2,1)}, bf16[1024,512]{1,0:T(8,128)(2,1)}, bf16[512,512]{1,0:T(8,128)(2,1)}, bf16[512...) custom-call(s32[64]{0:T(128)} %convert_reduce_fusion.meta_ref, s32[32]{0:T(128)} %ends_ref.3, bf16[1024,512]{1,0:T(8,128)(2,1)} %k_ref.1, ...), custom_call_target="tpu_custom_call" | custom-call | tf_op jit(solution)/shard_map/finish/pallas_call | solution.py:931
  (1 shorter events, 0.0 us)

commit v3 on v2

--- a/solution.py
+++ b/solution.py
@@ -39,8 +39,16 @@
     return lax.dot_general(a, b, (((0,), (0,)), ((), ())), preferred_element_type=F32)
 
 
-def local_ends(meta_ref, ends_ref, slab, width, count):
-    first = meta_ref[slab]
+def counts_of(ends_ref, marks):
+    def one(at, held):
+        end = ends_ref[at]
+        return tuple(count + (end <= mark).astype(jnp.int32) for count, mark in zip(held, marks))
+
+    zero = jnp.int32(0)
+    return lax.fori_loop(0, ends_ref.shape[0], one, (zero,) * len(marks), unroll=True)
+
+
+def local_ends(first, ends_ref, slab, width):
     last = ends_ref.shape[0] - 1
     end0 = ends_ref[jnp.minimum(first, last)] - slab * width
     end1 = jnp.where(
@@ -139,6 +147,103 @@
             copy.wait_send()
 
 
+class SplitSpread(Spread):
+    LEGS = 4
+
+    @staticmethod
+    def scratch(rows, kind):
+        each = rows // 2
+        return [
+            pltpu.VMEM((RING, HALF, rows, E, E), kind),
+            pltpu.VMEM((2, rows, E, E), F32),
+            pltpu.VMEM((HALF, rows, E, E), kind),
+            pltpu.VMEM((2, 2, HALF, each, E, E), kind),
+            pltpu.VMEM((HALF, each, E, E), kind),
+            pltpu.VMEM((HALF, each, E, E), kind),
+            pltpu.SemaphoreType.DMA((3,)),
+            pltpu.SemaphoreType.DMA((3,)),
+            pltpu.SemaphoreType.DMA((SplitSpread.LEGS, 2)),
+            pltpu.SemaphoreType.DMA((SplitSpread.LEGS, 2)),
+        ]
+
+    def __init__(self, place, rows, scratch, term):
+        self.rows, self.term, self.place = rows, term, place
+        self.parts, self.exact, self.passed, self.arrived, self.mail, self.mailed = scratch[:6]
+        send, recv, leg_send, leg_recv = scratch[6:]
+        left, right = place.neighbour(0, RING - 1), place.neighbour(0, 1)
+        each = rows // 2
+        self.far = [
+            remote_copy(self.parts.at[2, 0], self.passed.at[0], send.at[0], recv.at[0], left),
+            remote_copy(self.parts.at[2, 1], self.passed.at[1], send.at[1], recv.at[1], right),
+        ]
+        self.swap = remote_copy(self.mail, self.mailed, send.at[2], recv.at[2], place.partner())
+        self.legs, self.awaited = [], []
+        for leg, (m, i, side) in enumerate(((3, 1, 0), (1, 0, 1), (3, 0, 0), (1, 1, 1))):
+            chip = place.chip_at(0, m)
+            self.legs.append([])
+            for cd in range(2):
+                src = self.parts.at[m, i, pl.ds(each * cd, each)]
+                self.legs[-1].append(
+                    remote_copy(
+                        src,
+                        self.arrived.at[place.core, side, i],
+                        leg_send.at[leg, cd],
+                        leg_recv.at[leg, place.core],
+                        (chip + cd, place.head),
+                    )
+                )
+                self.awaited.append(
+                    remote_copy(
+                        src,
+                        self.arrived.at[cd, side, i],
+                        leg_send.at[leg, cd],
+                        leg_recv.at[leg, cd],
+                        (chip + cd, place.head),
+                    )
+                )
+
+    def begin(self):
+        for at, (m, i) in enumerate(((2, 0), (2, 1), (3, 1), (1, 0))):
+            for r in range(self.rows):
+                self.parts[m, i, r] = self.term(m, i, r).astype(self.parts.dtype)
+            for copy in self.far[at : at + 1] if at < 2 else self.legs[at - 2]:
+                copy.start()
+        each = self.rows // 2
+        for i in range(HALF):
+            for r in range(each):
+                self.mail[i, r] = self.term(0, i, each * (1 - self.place.core) + r)
+        self.swap.start()
+
+    def pass_on(self):
+        for at, (m, i) in enumerate(((3, 0), (1, 1))):
+            for r in range(self.rows):
+                self.exact[at, r] = self.term(m, i, r).astype(F32)
+        for at, (m, i) in enumerate(((3, 0), (1, 1))):
+            self.far[at].wait_recv()
+            for r in range(self.rows):
+                self.parts[m, i, r] = (
+                    self.exact[at, r] + self.passed[i, r].astype(F32)
+                ).astype(self.parts.dtype)
+            for copy in self.legs[2 + at]:
+                copy.start()
+
+    def arrive(self):
+        self.swap.wait_recv()
+        for copy in self.awaited:
+            copy.wait_recv()
+
+    def result(self, i, r, own):
+        each = self.rows // 2
+        core = self.place.core
+        side = core if own else 1 - core
+        base = self.term(0, i, each * core + r) if own else self.mailed[i, r]
+        return base + self.arrived[side, 0, i, r] + self.arrived[side, 1, i, r]
+
+    def finish(self):
+        for copy in self.far + [self.swap] + self.legs[0] + self.legs[1] + self.legs[2] + self.legs[3]:
+            copy.wait_send()
+
+
 class Gather:
     COPIES = 6
 
@@ -193,7 +298,6 @@
 
 
 def main_kernel(
-    meta_ref,
     ends_ref,
     cand_ref,
     lens_ref,
@@ -236,8 +340,6 @@
     qg_theirs,
     qg_mail,
     states,
-    states_mail,
-    states_in,
     carry_mail,
     carry_in,
     carry,
@@ -258,6 +360,10 @@
     gathered_qg,
     gathered_grads,
     table_ref,
+    firsts_ref,
+    lasts_ref,
+    dk_out,
+    dv_out,
     in_sem,
     out_sem,
     swap_send,
@@ -272,7 +378,7 @@
 ):
     place = Place()
     core = place.core
-    slabs = meta_ref.shape[0] // 2
+    slabs = lax.axis_size("seq")
     planes = lax.axis_size("head")
     width = pq.shape[0]
     cand_width = cq.shape[0]
@@ -302,7 +408,8 @@
     ]
     loads[0].start()
     loads[1].start()
-    lax.fori_loop(1, slabs, hello, 0)
+    lax.fori_loop(slabs // 2, slabs, hello, 0)
+    lax.fori_loop(1, slabs // 2, hello, 0)
     planes_other = [(place.seq, (place.head + at) % planes) for at in range(1, planes)]
     for device in planes_other:
         pl.semaphore_signal(barrier, inc=1, device_id=device, device_id_type=MESH)
@@ -315,7 +422,14 @@
     def swap(at, src, dst):
         return remote_copy(src, dst, swap_send.at[at], swap_recv.at[at], place.partner())
 
-    end0, end1 = local_ends(meta_ref, ends_ref, place.seq, width, PIECES)
+    chip = place.chip_at(0, 0)
+    seam_at = (chip + 1) * width
+    first0, last0, first1, last1 = counts_of(
+        ends_ref, (chip * width, seam_at - 1, seam_at, seam_at + width - 1)
+    )
+    end0, end1 = local_ends(
+        jnp.where(core == 0, first0, first1), ends_ref, place.seq, width
+    )
     spot = lax.broadcasted_iota(jnp.int32, (width, E), 0)
     masks[0] = flag(spot < end0).astype(BF)
     masks[1] = flag(jnp.logical_and(spot >= end0, spot < end1)).astype(BF)
@@ -335,10 +449,10 @@
         sums = piece_sums(HALF * (1 - core) + i)
         for j in range(PIECES):
             mail[i, j] = sums[:, j * E : (j + 1) * E]
-        if i == 0:
-            pl.semaphore_wait(barrier, slabs - 1 + planes - 1)
         pieces_swaps.append(swap(6 * i, mail.at[i], theirs.at[i, pl.ds(0, PIECES)]))
-        pieces_swaps[-1].start()
+    pl.semaphore_wait(barrier, slabs - 1 + planes - 1)
+    for copy in pieces_swaps:
+        copy.start()
     for i in range(HALF):
         sums = piece_sums(HALF * core + i)
         for j in range(PIECES):
@@ -350,9 +464,6 @@
             gathered_wide[k, i, 2] = jnp.zeros((E, E), F32)
             gathered_grads[k, i, NONE] = jnp.zeros((E, E), BF)
 
-    chip = place.chip_at(0, 0)
-    first0, first1 = meta_ref[chip], meta_ref[chip + 1]
-    last0, last1 = meta_ref[slabs + chip], meta_ref[slabs + chip + 1]
     off = jnp.clip(first1 - first0, 0, PIECES - 1)
     off_own, off_theirs = off * core, off * (1 - core)
 
@@ -389,6 +500,19 @@
         for j in range(1, CHIP_ENDS):
             gathered[0, i, j - 1] = chip_row(i, j).astype(BF)
     ends_ring.begin()
+
+    def count_chip(at, held):
+        start = at * 2 * width
+        firsts_ref[at], lasts_ref[at] = counts_of(ends_ref, (start, start + 2 * width - 1))
+        return held
+
+    lax.fori_loop(0, slabs // 2, count_chip, 0)
+
+    def first_of(seq):
+        return firsts_ref[seq // 2]
+
+    def last_of(seq):
+        return lasts_ref[seq // 2]
 
     def segment_of(at):
         return (at >= end0).astype(jnp.int32) + (at >= end1).astype(jnp.int32)
@@ -486,7 +610,7 @@
         total = None
         for k in range(RING):
             src = place.chip_at(k, 0)
-            same = jnp.logical_and(meta_ref[slabs + src + 1] == meta_ref[dest], src < dest)
+            same = jnp.logical_and(last_of(src) == first_of(dest), src < dest)
             term = gathered_wide[k, i, jnp.where(same, 1, 2)]
             total = term if total is None else total + term
         return total
@@ -498,7 +622,7 @@
         total = None
         for k in range(RING):
             src = place.chip_at(k, 0)
-            same = jnp.logical_and(meta_ref[src] == meta_ref[slabs + dest + 1], src > dest)
+            same = jnp.logical_and(first_of(src) == last_of(dest), src > dest)
             term = flag(same) * gathered_qg[k, i]
             total = term if total is None else total + term
         return total
@@ -510,18 +634,18 @@
         src_a = jnp.where(core == 0, src_z, src_x)
         src_b = jnp.where(core == 0, src_x, src_z)
         k_end = (src_a - place.pos_a + RING) % RING
-        row = wanted - meta_ref[2 * source]
+        row = wanted - first_of(2 * source)
         inner = jnp.logical_and(src_b == place.pos_b, row > 0)
         total = gathered[k_end, i, jnp.where(inner, jnp.minimum(row - 1, CHIP_ENDS - 2), CHIP_ENDS - 1)].astype(F32)
         for k in range(RING):
             src = place.chip_at(k, 0)
-            opens = jnp.logical_and(src < 2 * source, meta_ref[slabs + src + 1] == wanted)
+            opens = jnp.logical_and(src < 2 * source, last_of(src) == wanted)
             ends = jnp.logical_and(src == 2 * source, row == 0)
             total = total + gathered_wide[k, i, jnp.where(opens, 1, jnp.where(ends, 0, 2))]
         return total
 
     def grad_term(m, i, r):
-        wanted = meta_ref[place.chip_at(0, m)] + r
+        wanted = first_of(place.chip_at(0, m)) + r
         total = None
         for k in range(RING):
             src = 2 * place.chip_at(k, 0)
@@ -532,40 +656,30 @@
             total = term if total is None else total + term
         return total
 
-    to_states = Spread(place, 4, spread_scratch[:6], state_term)
-    to_memory = Spread(place, 2, spread_scratch[6:12], memory_term)
-    to_grads = Spread(place, CHIP_ROWS, spread_scratch[12:], grad_term)
+    to_states = SplitSpread(place, 4, spread_scratch[:10], state_term)
+    to_memory = Spread(place, 2, spread_scratch[10:16], memory_term)
+    to_grads = Spread(place, CHIP_ROWS, spread_scratch[16:], grad_term)
 
     qg_swap.wait()
     own_scale = jnp.where(core == 0, 1.0, whole)
     their_scale = jnp.where(core == 0, whole, 1.0)
     for i in range(HALF):
         gathered_qg[0, i] = own_scale * qg_own[i] + their_scale * qg_theirs[i]
+    qg_ring = Gather(place, lambda k, i: gathered_qg.at[k, i], ring_send.at[2], ring_recv.at[2])
     wide_ring.arrive()
     ends_ring.arrive()
+    qg_ring.begin()
     to_states.begin()
     cand_near(0, 2)
     to_states.pass_on()
-    qg_ring = Gather(place, lambda k, i: gathered_qg.at[k, i], ring_send.at[2], ring_recv.at[2])
-    qg_ring.begin()
+    qg_ring.pass_on()
     cand_near(2, 4)
-    qg_ring.pass_on()
     prompt_task(3, 3, 4)
     to_states.arrive()
     for i in range(HALF):
         for r in range(2):
-            states_mail[i, r] = to_states.result(i, 2 * (1 - core) + r).astype(BF)
-    states_swap = swap(2, states_mail, states_in)
-    states_swap.start()
-    for i in range(HALF):
-        for r in range(2):
-            states[r, HALF * core + i] = to_states.result(i, 2 * core + r).astype(BF)
-    qg_ring.arrive()
-    to_memory.begin()
-    states_swap.wait()
-    for i in range(HALF):
-        for r in range(2):
-            states[r, HALF * (1 - core) + i] = states_in[i, r]
+            states[r, HALF * core + i] = to_states.result(i, r, True).astype(BF)
+            states[r, HALF * (1 - core) + i] = to_states.result(i, r, False).astype(BF)
 
     sum_all = jnp.zeros((1, E), F32)
     sum_second = jnp.zeros((1, E), F32)
@@ -594,7 +708,9 @@
     for copy in to_planes:
         copy.start()
     heads_ref[place.head] = mine_ref[...]
-    to_memory.pass_on()
+    qg_ring.arrive()
+    to_memory.begin()
+    prompt_task(2, 0, 2)
     for copy in to_planes:
         copy.wait()
     total = heads_ref[0]
@@ -632,10 +748,12 @@
         for at, plane in enumerate(lax.fori_loop(0, slabs, one, (blank,) * 4)):
             table_ref[at] = plane
 
-    lax.fori_loop(1, slabs, tell, 0)
+    lax.fori_loop(slabs // 2, slabs, tell, 0)
+    lax.fori_loop(1, slabs // 2, tell, 0)
     scores_ref[place.seq] = total
     build_table()
-    prompt_task(2, 0, 3)
+    to_memory.pass_on()
+    prompt_task(2, 2, 4)
     lax.fori_loop(1, slabs, told, 0)
 
     raw = scores_ref[...].reshape(slabs, E)
@@ -722,6 +840,7 @@
     cand_backward(0, 2)
     grads_ring.pass_on()
     cand_backward(2, 4)
+    prompt_task(1, 0, 2)
     outputs = [store(0, cdq, cdq_hbm), store(1, cdk, cdk_hbm), store(2, cdv, cdv_hbm)]
     carry_swap.wait()
     for i in range(HALF):
@@ -735,11 +854,12 @@
                     + gathered_grads[k, i, source + 1].astype(F32)
                 ).astype(BF)
     to_grads.begin()
+    prompt_task(1, 2, 4)
     to_grads.pass_on()
-    prompt_task(2, 3, 4)
-    prompt_task(1, 0, 4)
     prompt_task(0, 0, 4)
-    outputs += [store(3, dkp, dkp_hbm), store(4, dvp, dvp_hbm)]
+    dk_out[...] = dkp[...].astype(BF)
+    dv_out[...] = dvp[...].astype(BF)
+    outputs += [store(3, dk_out, dkp_hbm), store(4, dv_out, dvp_hbm)]
     dq_finish()
     outputs.append(store(5, dq_out, dq_hbm))
     to_grads.arrive()
@@ -778,7 +898,6 @@
 
 
 def last_kernel(
-    meta_ref,
     ends_ref,
     k_ref,
     v_ref,
@@ -798,14 +917,15 @@
 ):
     width = k_ref.shape[0]
     slab = lax.axis_index("seq")
-    end0, end1 = local_ends(meta_ref, ends_ref, slab, width, PIECES)
+    first = counts_of(ends_ref, (slab * width,))[0]
+    end0, end1 = local_ends(first, ends_ref, slab, width)
     spot = lax.broadcasted_iota(jnp.int32, (width, 1), 0)
     k, v = k_ref[...], v_ref[...]
     dk = [dot_nt(v, right_ref[j, 0]) for j in range(PIECES)]
     dv = [dot_nn(k, right_ref[j, 0]) for j in range(PIECES)]
     for out, part, far in ((dk_ref, dkp_ref, dk), (dv_ref, dvp_ref, dv)):
         chosen = jnp.where(spot < end0, far[0], jnp.where(spot < end1, far[1], far[2]))
-        out[...] = (part[...] + chosen).astype(BF)
+        out[...] = (part[...].astype(F32) + chosen).astype(BF)
     dq_ref[...] = dq_in[...]
     cdq_ref[...] = cdq_in[...]
     cdk_ref[...] = cdk_in[...]
@@ -830,12 +950,8 @@
     width = prompt_q.shape[0]
     cand_width = cand_q.shape[0]
     flat = prompt_q.shape[1]
-    starts = jnp.arange(slabs, dtype=jnp.int32) * width
-    marks = jnp.concatenate([starts, starts + (width - 1)])
-    meta = jnp.sum((prompt_ends[None, :] <= marks[:, None]).astype(jnp.int32), axis=1)
     any_spec = pl.BlockSpec(memory_space=pl.ANY)
     prompt_shape = jax.ShapeDtypeStruct((width, flat), BF)
-    prompt_wide = jax.ShapeDtypeStruct((width, flat), F32)
     cand_shape = jax.ShapeDtypeStruct((cand_width, flat), BF)
     prompt_buf = pltpu.VMEM((width, flat), BF)
     prompt_acc = pltpu.VMEM((width, flat), F32)
@@ -846,15 +962,15 @@
         main_kernel,
         out_shape=(
             prompt_shape,
-            prompt_wide,
-            prompt_wide,
+            prompt_shape,
+            prompt_shape,
             cand_shape,
             cand_shape,
             cand_shape,
             jax.ShapeDtypeStruct((PIECES, LOCAL_HEADS, E, E), BF),
             jax.ShapeDtypeStruct((1, 1), F32),
         ),
-        in_specs=[SMEM_SPEC] * 5 + [VMEM_SPEC] + [any_spec] * 7,
+        in_specs=[SMEM_SPEC] * 4 + [VMEM_SPEC] + [any_spec] * 7,
         out_specs=[any_spec] * 6 + [VMEM_SPEC] * 2,
         scratch_shapes=[prompt_buf] * 4
         + [cand_buf] * 3
@@ -870,8 +986,6 @@
             half_rows(HALF, kind=F32),
             half_rows(HALF, kind=F32),
             half_rows(2, LOCAL_HEADS),
-            half_rows(HALF, 2),
-            half_rows(HALF, 2),
             half_rows(HALF),
             half_rows(HALF),
             half_rows(LOCAL_HEADS),
@@ -892,6 +1006,10 @@
             half_rows(RING, HALF, kind=F32),
             half_rows(RING, HALF, NONE + 1),
             pltpu.VMEM((4, slabs, E), jnp.int32),
+            pltpu.SMEM((slabs // 2,), jnp.int32),
+            pltpu.SMEM((slabs // 2,), jnp.int32),
+            prompt_buf,
+            prompt_buf,
             dma((7,)),
             dma((6,)),
             dma((7,)),
@@ -903,7 +1021,7 @@
             dma((slabs,)),
             dma((slabs,)),
         ]
-        + Spread.scratch(4, F32)
+        + SplitSpread.scratch(4, F32)
         + Spread.scratch(2, F32)
         + Spread.scratch(CHIP_ROWS, BF),
         compiler_params=pltpu.CompilerParams(
@@ -911,7 +1029,6 @@
         ),
         name="exchange",
     )(
-        meta,
         prompt_ends,
         cand_prompt,
         cand_lengths,
@@ -932,14 +1049,13 @@
         last_kernel,
         grid=(LOCAL_HEADS,),
         out_shape=(prompt_shape,) * 3 + (cand_shape,) * 3,
-        in_specs=[SMEM_SPEC] * 2
+        in_specs=[SMEM_SPEC]
         + [prompt_block] * 4
         + [pl.BlockSpec((PIECES, 1, E, E), lambda h: (0, h, 0, 0)), prompt_block]
         + [cand_block] * 3,
         out_specs=(prompt_block,) * 3 + (cand_block,) * 3,
         name="finish",
     )(
-        meta,
         prompt_ends,
         prompt_k,
         prompt_v,

time: 83.6 us -> 77 us (0.921)
  Pallas kernels: 79.6 us -> 74.4 us
  other arithmetic: 1.33 us -> 0 us
    pallas_call x1, Pallas kernels: 72.7 us -> 67.8 us  [per_device(): pl.pallas_call(main_kernel, out_shape=(prompt_shape, prompt_shape, prompt...]
    reduce_sum x1 -> x0, other arithmetic: 1.25 us -> none  [per_device(): jnp.sum((prompt_ends[None, :] <= marks[:, None]).astype(jnp.int32), axis=1)]
where the time goes in v3:
time: 77 us; the launch traced here: 76.8 us
  Pallas kernels  74.4 us (97%)
  between operations  2.45 us (3%)
    pallas_call x1, Pallas kernels, per_device(): pl.pallas_call(main_kernel, out_shape=(prompt_shape, prompt_shape, prompt...  67.8 us
    pallas_call x1, Pallas kernels, per_device(): pl.pallas_call(last_kernel, grid=(LOCAL_HEADS,), out_shape=(prompt_shape,...  6.53 us

profile of v3, /device:TPU:1, one launch (start us, length us, event | category | flops | bytes accessed | tf_op | source)
XLA Modules:
  0.0 76.8 jit_solution(4165521270553711715)
XLA Ops:
  0.6 67.8 %exchange.1 = (bf16[1024,512]{1,0:T(8,128)(2,1)}, bf16[1024,512]{1,0:T(8,128)(2,1)}, bf16[1024,512]{1,0:T(8,128)(2,1)}, bf16[512,512]{1,0:T(8,128)(2,1)}, bf16[5...) custom-call(s32[32]{0:T(128)} %ends_ref.3, s32[64]{0:T(128)} %cand_ref.1, ...), custom_call_target="tpu_custom_call" | custom-call | tf_op jit(solution)/shard_map/exchange/pallas_call | solution.py:961
  68.5 6.5 %finish.1 = (bf16[1024,512]{1,0:T(8,128)(2,1)}, bf16[1024,512]{1,0:T(8,128)(2,1)}, bf16[1024,512]{1,0:T(8,128)(2,1)}, bf16[512,512]{1,0:T(8,128)(2,1)}, bf16[512...) custom-call(s32[32]{0:T(128)} %ends_ref.3, bf16[1024,512]{1,0:T(8,128)(2,1)} %k_ref.1, bf16[1024,512]{1,0:T(8,128)(2,1)} %v_ref.1, ...), custom_call_target="tpu_custom_call" | custom-call | tf_op jit(solution)/shard_map/finish/pallas_call | solution.py:1048

commit v4 on v3

--- a/solution.py
+++ b/solution.py
@@ -14,7 +14,6 @@
 RING = 4
 CHUNK = 256
 PIECES = 3
-CHIP_ROWS = 5
 CHIP_ENDS = 4
 SUM01, SUM23, NONE = 4, 5, 6
 FAR = 1 << 30
@@ -158,8 +157,8 @@
             pltpu.VMEM((2, rows, E, E), F32),
             pltpu.VMEM((HALF, rows, E, E), kind),
             pltpu.VMEM((2, 2, HALF, each, E, E), kind),
-            pltpu.VMEM((HALF, each, E, E), kind),
-            pltpu.VMEM((HALF, each, E, E), kind),
+            pltpu.VMEM((HALF, each, E, E), F32),
+            pltpu.VMEM((HALF, each, E, E), F32),
             pltpu.SemaphoreType.DMA((3,)),
             pltpu.SemaphoreType.DMA((3,)),
             pltpu.SemaphoreType.DMA((SplitSpread.LEGS, 2)),
@@ -203,21 +202,22 @@
                 )
 
     def begin(self):
+        each = self.rows // 2
         for at, (m, i) in enumerate(((2, 0), (2, 1), (3, 1), (1, 0))):
             for r in range(self.rows):
-                self.parts[m, i, r] = self.term(m, i, r).astype(self.parts.dtype)
+                self.parts[m, i, r] = self.term(m, i, *divmod(r, each)).astype(self.parts.dtype)
             for copy in self.far[at : at + 1] if at < 2 else self.legs[at - 2]:
                 copy.start()
-        each = self.rows // 2
         for i in range(HALF):
             for r in range(each):
-                self.mail[i, r] = self.term(0, i, each * (1 - self.place.core) + r)
+                self.mail[i, r] = self.term(0, i, 1 - self.place.core, r)
         self.swap.start()
 
     def pass_on(self):
+        each = self.rows // 2
         for at, (m, i) in enumerate(((3, 0), (1, 1))):
             for r in range(self.rows):
-                self.exact[at, r] = self.term(m, i, r).astype(F32)
+                self.exact[at, r] = self.term(m, i, *divmod(r, each))
         for at, (m, i) in enumerate(((3, 0), (1, 1))):
             self.far[at].wait_recv()
             for r in range(self.rows):
@@ -233,11 +233,10 @@
             copy.wait_recv()
 
     def result(self, i, r, own):
-        each = self.rows // 2
         core = self.place.core
         side = core if own else 1 - core
-        base = self.term(0, i, each * core + r) if own else self.mailed[i, r]
-        return base + self.arrived[side, 0, i, r] + self.arrived[side, 1, i, r]
+        base = self.term(0, i, core, r) if own else self.mailed[i, r]
+        return base + self.arrived[side, 0, i, r].astype(F32) + self.arrived[side, 1, i, r].astype(F32)
 
     def finish(self):
         for copy in self.far + [self.swap] + self.legs[0] + self.legs[1] + self.legs[2] + self.legs[3]:
@@ -275,6 +274,66 @@
         for copy in self.copies[2:]:
             copy.wait_recv()
         for copy in self.copies:
+            copy.wait_send()
+
+
+class CrossGather:
+    def __init__(self, place, mail, slot, block, scratch):
+        send, recv, on_send, on_recv = scratch
+        core = place.core
+        hops = ((0, RING - 1, 1), (1, 1, 3), (1, RING - 1, 1), (0, 1, 3))
+        self.near, self.cross, self.awaited = [], [], []
+        for at, (i, move, k) in enumerate(hops):
+            near = place.neighbour(move, 0)
+            other = (place.chip_at(0, move) + 1 - core, place.head)
+            self.near.append(
+                remote_copy(
+                    slot(0, i, core), slot(k, i, core), send.at[at, 0], recv.at[at, core], near
+                )
+            )
+            self.cross.append(
+                remote_copy(mail(i), slot(k, i, core), send.at[at, 1], recv.at[at, core], other)
+            )
+            self.awaited.append(
+                [
+                    remote_copy(
+                        slot(0, i, cd), slot(k, i, cd), send.at[at, 0], recv.at[at, cd], near
+                    )
+                    for cd in range(2)
+                ]
+            )
+        self.onward = [
+            remote_copy(
+                block(1, 0),
+                block(2, 0),
+                on_send.at[0],
+                on_recv.at[0],
+                place.neighbour(RING - 1, 0),
+            ),
+            remote_copy(
+                block(3, 1), block(2, 1), on_send.at[1], on_recv.at[1], place.neighbour(1, 0)
+            ),
+        ]
+
+    def begin(self, copies):
+        for copy in copies:
+            copy.start()
+
+    def take(self, at):
+        for copy in self.awaited[at]:
+            copy.wait_recv()
+
+    def pass_on(self):
+        for at in range(2):
+            self.take(at)
+            self.onward[at].start()
+
+    def arrive(self):
+        self.take(2)
+        self.take(3)
+        for copy in self.onward:
+            copy.wait_recv()
+        for copy in self.near + self.cross + self.onward:
             copy.wait_send()
 
 
@@ -344,9 +403,8 @@
     carry_in,
     carry,
     chip_carry,
-    right_sum,
-    right_mail,
-    right_in,
+    later_mail,
+    later_in,
     attn_ref,
     outs_ref,
     dout_ref,
@@ -361,6 +419,7 @@
     gathered_grads,
     table_ref,
     firsts_ref,
+    seconds_ref,
     lasts_ref,
     dk_out,
     dv_out,
@@ -374,6 +433,10 @@
     y_recv,
     s_send,
     s_recv,
+    cross_send,
+    cross_recv,
+    onward_send,
+    onward_recv,
     *spread_scratch,
 ):
     place = Place()
@@ -503,7 +566,9 @@
 
     def count_chip(at, held):
         start = at * 2 * width
-        firsts_ref[at], lasts_ref[at] = counts_of(ends_ref, (start, start + 2 * width - 1))
+        firsts_ref[at], seconds_ref[at], lasts_ref[at] = counts_of(
+            ends_ref, (start, start + width, start + 2 * width - 1)
+        )
         return held
 
     lax.fori_loop(0, slabs // 2, count_chip, 0)
@@ -627,8 +692,8 @@
             total = term if total is None else total + term
         return total
 
-    def state_term(m, i, r):
-        wanted = cand_ref[2 * place.chip_at(0, m) + r]
+    def state_term(m, i, cd, r):
+        wanted = cand_ref[2 * (place.chip_at(0, m) + cd) + r]
         source = jnp.clip((ends_ref[wanted] - 1) // (2 * width), 0, slabs // 2 - 1)
         src_z, src_x = source // RING, source % RING
         src_a = jnp.where(core == 0, src_z, src_x)
@@ -644,8 +709,9 @@
             total = total + gathered_wide[k, i, jnp.where(opens, 1, jnp.where(ends, 0, 2))]
         return total
 
-    def grad_term(m, i, r):
-        wanted = first_of(place.chip_at(0, m)) + r
+    def grad_term(m, i, cd, j):
+        at = place.chip_at(0, m) // 2
+        wanted = jnp.where(cd == 0, firsts_ref[at], seconds_ref[at]) + j
         total = None
         for k in range(RING):
             src = 2 * place.chip_at(k, 0)
@@ -658,7 +724,7 @@
 
     to_states = SplitSpread(place, 4, spread_scratch[:10], state_term)
     to_memory = Spread(place, 2, spread_scratch[10:16], memory_term)
-    to_grads = Spread(place, CHIP_ROWS, spread_scratch[16:], grad_term)
+    to_grads = SplitSpread(place, 2 * PIECES, spread_scratch[16:], grad_term)
 
     qg_swap.wait()
     own_scale = jnp.where(core == 0, 1.0, whole)
@@ -807,19 +873,21 @@
             grads_mail[i, r] = sums[:, r * E : (r + 1) * E].astype(BF)
     own_slots = pl.ds(2 * core, 2)
     grads_swap = swap(3, grads_mail, gathered_grads.at[0, :, own_slots])
+    grads_ring = CrossGather(
+        place,
+        lambda i: grads_mail.at[i],
+        lambda k, i, cd: gathered_grads.at[k, i, pl.ds(2 * cd, 2)],
+        lambda k, i: gathered_grads.at[k, i, pl.ds(0, 4)],
+        (cross_send, cross_recv, onward_send, onward_recv),
+    )
+    grads_ring.begin(grads_ring.cross)
     grads_swap.start()
     for i in range(HALF):
         sums = grad_sums(HALF * core + i)
         for r in range(2):
             gathered_grads[0, i, 2 * core + r] = sums[:, r * E : (r + 1) * E].astype(BF)
+    grads_ring.begin(grads_ring.near)
     grads_swap.wait()
-    grads_ring = Gather(
-        place,
-        lambda k, i: gathered_grads.at[k, i, pl.ds(0, 4)],
-        ring_send.at[3],
-        ring_recv.at[3],
-    )
-    grads_ring.begin()
 
     to_memory.arrive()
     seam = slot_in(off, PIECES)
@@ -830,11 +898,20 @@
         keep = jnp.where(at_core == 0, 1.0, whole)
         return (keep * chip_carry[i] + is_second * before).astype(BF)
 
-    for i in range(HALF):
+    def later_row(i, at_core):
+        chip_later = to_memory.result(i, 1)
+        second_qg = jnp.where(core == 0, qg_theirs[i], qg_own[i])
+        inner = flag(first1 == last0) * second_qg + flag(last1 == last0) * chip_later
+        return jnp.where(at_core == 0, inner, chip_later)
+
+    for i in range(HALF):
+        later_mail[i] = later_row(i, 1 - core)
         chip_carry[i] = to_memory.result(i, 0)
         carry_mail[i] = carry_row(i, 1 - core)
     carry_swap = swap(4, carry_mail, carry_in)
+    later_swap = swap(5, later_mail, later_in)
     carry_swap.start()
+    later_swap.start()
     for i in range(HALF):
         carry[HALF * core + i] = carry_row(i, core)
     cand_backward(0, 2)
@@ -843,6 +920,7 @@
     prompt_task(1, 0, 2)
     outputs = [store(0, cdq, cdq_hbm), store(1, cdk, cdk_hbm), store(2, cdv, cdv_hbm)]
     carry_swap.wait()
+    later_swap.wait()
     for i in range(HALF):
         carry[HALF * (1 - core) + i] = carry_in[i]
     grads_ring.arrive()
@@ -863,36 +941,16 @@
     dq_finish()
     outputs.append(store(5, dq_out, dq_hbm))
     to_grads.arrive()
-    for i in range(HALF):
-        for r in range(CHIP_ROWS):
-            right_sum[r, i] = to_grads.result(i, r)
-
-    def later_row(i, at_core):
-        chip_later = to_memory.result(i, 1)
-        second_qg = jnp.where(core == 0, qg_theirs[i], qg_own[i])
-        inner = flag(first1 == last0) * second_qg + flag(last1 == last0) * chip_later
-        return jnp.where(at_core == 0, inner, chip_later)
-
-    def right_row(i, j, at_core, later):
-        into = jnp.where(at_core == 0, last0 - first0, last1 - first1)
-        return (right_sum[j + off * at_core, i] + flag(into == j) * later).astype(BF)
-
-    for i in range(HALF):
-        later = later_row(i, 1 - core)
-        for j in range(PIECES):
-            right_mail[j, i] = right_row(i, j, 1 - core, later)
-    right_swap = swap(5, right_mail, right_in)
-    right_swap.start()
-    for i in range(HALF):
-        later = later_row(i, core)
-        for j in range(PIECES):
-            right_ref[j, HALF * core + i] = right_row(i, j, core, later)
+    into = jnp.where(core == 0, last0 - first0, last1 - first1)
+    for i in range(HALF):
+        for side, own_side in ((core, True), (1 - core, False)):
+            later = later_row(i, core) if own_side else later_in[i]
+            for j in range(PIECES):
+                right_ref[j, HALF * side + i] = (
+                    to_grads.result(i, j, own_side) + flag(into == j) * later
+                ).astype(BF)
     for spread in (to_states, to_memory, to_grads):
         spread.finish()
-    right_swap.wait()
-    for i in range(HALF):
-        for j in range(PIECES):
-            right_ref[j, HALF * (1 - core) + i] = right_in[j, i]
     for copy in outputs:
         copy.wait()
 
@@ -921,9 +979,11 @@
     end0, end1 = local_ends(first, ends_ref, slab, width)
     spot = lax.broadcasted_iota(jnp.int32, (width, 1), 0)
     k, v = k_ref[...], v_ref[...]
-    dk = [dot_nt(v, right_ref[j, 0]) for j in range(PIECES)]
-    dv = [dot_nn(k, right_ref[j, 0]) for j in range(PIECES)]
-    for out, part, far in ((dk_ref, dkp_ref, dk), (dv_ref, dvp_ref, dv)):
+    rows = [right_ref[j, 0] for j in range(PIECES)]
+    dk = dot_nt(v, jnp.concatenate(rows, axis=0))
+    dv = dot_nn(k, jnp.concatenate(rows, axis=1))
+    for out, part, wide in ((dk_ref, dkp_ref, dk), (dv_ref, dvp_ref, dv)):
+        far = [wide[:, j * E : (j + 1) * E] for j in range(PIECES)]
         chosen = jnp.where(spot < end0, far[0], jnp.where(spot < end1, far[1], far[2]))
         out[...] = (part[...].astype(F32) + chosen).astype(BF)
     dq_ref[...] = dq_in[...]
@@ -990,9 +1050,8 @@
             half_rows(HALF),
             half_rows(LOCAL_HEADS),
             half_rows(HALF, kind=F32),
-            half_rows(CHIP_ROWS, HALF, kind=F32),
-            half_rows(PIECES, HALF),
-            half_rows(PIECES, HALF),
+            half_rows(HALF, kind=F32),
+            half_rows(HALF, kind=F32),
             pltpu.VMEM((LOCAL_HEADS, cand_width, cand_width), BF),
             pltpu.VMEM((LOCAL_HEADS, cand_width, E), F32),
             pltpu.VMEM((LOCAL_HEADS, cand_width, E), BF),
@@ -1008,6 +1067,7 @@
             pltpu.VMEM((4, slabs, E), jnp.int32),
             pltpu.SMEM((slabs // 2,), jnp.int32),
             pltpu.SMEM((slabs // 2,), jnp.int32),
+            pltpu.SMEM((slabs // 2,), jnp.int32),
             prompt_buf,
             prompt_buf,
             dma((7,)),
@@ -1020,10 +1080,14 @@
             dma((3,)),
             dma((slabs,)),
             dma((slabs,)),
+            dma((4, 2)),
+            dma((4, 2)),
+            dma((2,)),
+            dma((2,)),
         ]
         + SplitSpread.scratch(4, F32)
         + Spread.scratch(2, F32)
-        + Spread.scratch(CHIP_ROWS, BF),
+        + SplitSpread.scratch(2 * PIECES, BF),
         compiler_params=pltpu.CompilerParams(
             collective_id=0, has_side_effects=True, vmem_limit_bytes=56 << 20
         ),

time: 77 us -> 75.2 us (0.977)
  Pallas kernels: 74.4 us -> 72.5 us
    pallas_call x1, Pallas kernels: 67.8 us -> 66 us  [per_device(): pl.pallas_call(main_kernel, out_shape=(prompt_shape, prompt_shape, prompt...]
where the time goes in v4:
time: 75.2 us; the launch traced here: 74.9 us
  Pallas kernels  72.5 us (96%)
  between operations  2.45 us (3%)
    pallas_call x1, Pallas kernels, per_device(): pl.pallas_call(main_kernel, out_shape=(prompt_shape, prompt_shape, prompt...  66 us
    pallas_call x1, Pallas kernels, per_device(): pl.pallas_call(last_kernel, grid=(LOCAL_HEADS,), out_shape=(prompt_shape,...  6.42 us

profile of v4, /device:TPU:1, one launch (start us, length us, event | category | flops | bytes accessed | tf_op | source)
XLA Modules:
  0.0 74.9 jit_solution(310453397869065361)
XLA Ops:
  0.6 66.0 %exchange.1 = (bf16[1024,512]{1,0:T(8,128)(2,1)}, bf16[1024,512]{1,0:T(8,128)(2,1)}, bf16[1024,512]{1,0:T(8,128)(2,1)}, bf16[512,512]{1,0:T(8,128)(2,1)}, bf16[5...) custom-call(s32[32]{0:T(128)} %ends_ref.3, s32[64]{0:T(128)} %cand_ref.1, ...), custom_call_target="tpu_custom_call" | custom-call | tf_op jit(solution)/shard_map/exchange/pallas_call | solution.py:1021
  66.7 6.4 %finish.1 = (bf16[1024,512]{1,0:T(8,128)(2,1)}, bf16[1024,512]{1,0:T(8,128)(2,1)}, bf16[1024,512]{1,0:T(8,128)(2,1)}, bf16[512,512]{1,0:T(8,128)(2,1)}, bf16[512...) custom-call(s32[32]{0:T(128)} %ends_ref.3, bf16[1024,512]{1,0:T(8,128)(2,1)} %k_ref.1, bf16[1024,512]{1,0:T(8,128)(2,1)} %v_ref.1, ...), custom_call_target="tpu_custom_call" | custom-call | tf_op jit(solution)/shard_map/finish/pallas_call | solution.py:1112
